TPU v7x, 32 devices: a whole 2x2x4 slice. The times are simulated.
32 devices in a mesh: ens: 2 (over y), gx: 4 (over z), gy: 4 (over x, core).
Axes of the slice: x: 2, y: 2, z: 4, core: 2. Of those that a mesh axis runs over, the one named last changes fastest.
Arguments:
- log_cond: float32 [64, 512, 128], P(('ens', 'gx'), 'gy'), parts along dimension 0, may hold values from -1 to 1
- checkpoint: float32 [64, 512, 128], P(('ens', 'gx'), 'gy'), parts along dimension 0, may hold values from 0 to 1
- survey: float32 [64, 512, 128], P(('ens', 'gx'), 'gy'), parts along dimension 0, may hold values from 0 to 1
- survey_weight: float32 [64, 512, 128], P(('ens', 'gx'), 'gy'), parts along dimension 0, may hold values from 0.5 to 5
- well_cells: int32 [512], P('ens'), parts along dimension 0, may hold values from 0 to 2097151
- well_data: float32 [512], P('ens'), parts along dimension 0, may hold values from 0 to 1
- well_weight: float32 [512], P('ens'), parts along dimension 0, may hold values from 1 to 10
- source_cells: int32 [128], P('ens'), parts along dimension 0, may hold values from 0 to 2097151
- source_rate: float32 [128], P('ens'), parts along dimension 0, may hold values from 5 to 20
- step_number: int32 [2], P('ens'), parts along dimension 0, may hold values from 0 to 1999
Outputs:
- log_cond_grad: float32 [64, 512, 128], P(('ens', 'gx'), 'gy'), parts along dimension 0
- checkpoint_adjoint: float32 [64, 512, 128], P(('ens', 'gx'), 'gy'), parts along dimension 0
- concentration: float32 [64, 512, 128], P(('ens', 'gx'), 'gy'), parts along dimension 0
- misfit: float32 [2], P('ens'), parts along dimension 0
There are 2 independent parts, one for each index of `ens`. A program takes and returns all parts, laid end to end along the dimension named above; each array names one. Nothing has to cross between parts.
Inputs may be any that keep to these rules, and one draw needn't show every extreme that they name: `well_cells`: flat cell index (x * 512 + y) * 128 + z. `source_cells`: flat cell index (x * 512 + y) * 128 + z.
All inputs are finite; a program needn't handle non-finite values.
Results may differ from a plain program's by a relative error of at most 0.00002.
Values sent between devices are 32-bit elements; how exact they have to be, the bound alone decides.
A program may use at most 64 MiB of HBM per device.

v0:
```python
import jax
import jax.numpy as jnp
from jax import lax
from jax.sharding import PartitionSpec as P

time_step = 0.2
head_slope = 0.5
molecular = 0.05
dispersivity = 0.1


def extended(block, sides, width):
    for axis, dim in sides:
        count = lax.axis_size(axis)
        forward = [(i, i + 1) for i in range(count - 1)]
        backward = [(target, source) for source, target in forward]
        low = lax.ppermute(
            lax.slice_in_dim(block, block.shape[dim] - width, None, axis=dim), axis, forward
        )
        high = lax.ppermute(lax.slice_in_dim(block, 0, width, axis=dim), axis, backward)
        block = jnp.concatenate([low, block, high], axis=dim)
    return block


def validity(extent, rim_width, position, grid_total):
    global_pos = position * extent - rim_width + jnp.arange(extent + 2 * rim_width, dtype=jnp.int32)
    return ((global_pos >= 0) & (global_pos < grid_total)).astype(jnp.float32)


def face_terms(log_cond, mask_x, mask_y):
    cond_x = jnp.exp(0.5 * (log_cond[:-1] + log_cond[1:]))
    cond_y = jnp.exp(0.5 * (log_cond[:, :-1] + log_cond[:, 1:]))
    cond_z = jnp.exp(0.5 * (log_cond[:, :, :-1] + log_cond[:, :, 1:]))
    open_x = (mask_x[:-1] * mask_x[1:])[:, None, None]
    open_y = (mask_y[:-1] * mask_y[1:])[None, :, None]
    return (cond_x, cond_y, cond_z, open_x, open_y)


def forward_step(tracer, log_cond, mask_x, mask_y, source):
    cond_x, cond_y, cond_z, open_x, open_y = face_terms(log_cond, mask_x, mask_y)
    flux_x = open_x * (
        head_slope * cond_x * tracer[:-1]
        - (molecular + dispersivity * cond_x) * (tracer[1:] - tracer[:-1])
    )
    flux_y = open_y * (-(molecular + dispersivity * cond_y) * (tracer[:, 1:] - tracer[:, :-1]))
    flux_z = -(molecular + dispersivity * cond_z) * (tracer[:, :, 1:] - tracer[:, :, :-1])
    div_x = (flux_x[1:] - flux_x[:-1])[:, 1:-1]
    div_y = (flux_y[:, 1:] - flux_y[:, :-1])[1:-1]
    padded_z = jnp.pad(flux_z, ((0, 0), (0, 0), (1, 1)))
    div_z = (padded_z[:, :, 1:] - padded_z[:, :, :-1])[1:-1, 1:-1]
    return tracer[1:-1, 1:-1] - time_step * (div_x + div_y + div_z) + time_step * source[1:-1, 1:-1]


def adjoint_step(adjoint, tracer, log_cond, mask_x, mask_y):
    cond_x, cond_y, cond_z, open_x, open_y = face_terms(log_cond, mask_x, mask_y)
    disp_x = molecular + dispersivity * cond_x
    disp_y = molecular + dispersivity * cond_y
    disp_z = molecular + dispersivity * cond_z
    jump_x = open_x * time_step * (adjoint[1:] - adjoint[:-1])
    jump_y = open_y * time_step * (adjoint[:, 1:] - adjoint[:, :-1])
    jump_z = time_step * (adjoint[:, :, 1:] - adjoint[:, :, :-1])
    push_x = jump_x * (head_slope * cond_x + disp_x)
    pull_x = -jump_x * disp_x
    push_y = jump_y * disp_y
    pull_y = -jump_y * disp_y
    push_z = jnp.pad(jump_z * disp_z, ((0, 0), (0, 0), (1, 1)))
    pull_z = jnp.pad(-jump_z * disp_z, ((0, 0), (0, 0), (1, 1)))
    sens_x = (
        jump_x
        * (head_slope * tracer[:-1] - dispersivity * (tracer[1:] - tracer[:-1]))
        * 0.5
        * cond_x
    )
    sens_y = jump_y * (-dispersivity * (tracer[:, 1:] - tracer[:, :-1])) * 0.5 * cond_y
    sens_z = jnp.pad(
        jump_z * (-dispersivity * (tracer[:, :, 1:] - tracer[:, :, :-1])) * 0.5 * cond_z,
        ((0, 0), (0, 0), (1, 1)),
    )
    updated = (
        adjoint[1:-1, 1:-1]
        + (push_x[1:] + pull_x[:-1])[:, 1:-1]
        + (push_y[:, 1:] + pull_y[:, :-1])[1:-1]
    )
    updated = updated + (push_z[:, :, 1:] + pull_z[:, :, :-1])[1:-1, 1:-1]
    gradient = (sens_x[1:] + sens_x[:-1])[:, 1:-1] + (sens_y[:, 1:] + sens_y[:, :-1])[1:-1]
    gradient = gradient + (sens_z[:, :, 1:] + sens_z[:, :, :-1])[1:-1, 1:-1]
    return (updated, gradient)


def locate(cells, start_x, start_y, extent_x, extent_y, grid_y, grid_z):
    along_x = cells // (grid_y * grid_z) - start_x
    along_y = cells // grid_z % grid_y - start_y
    along_z = cells % grid_z
    inside = ((along_x >= 0) & (along_x < extent_x) & (along_y >= 0) & (along_y < extent_y)).astype(
        jnp.float32
    )
    return (jnp.clip(along_x, 0, extent_x - 1), jnp.clip(along_y, 0, extent_y - 1), along_z, inside)


def on_device(
    log_cond,
    checkpoint,
    survey,
    survey_weight,
    well_cells,
    well_data,
    well_weight,
    source_cells,
    source_rate,
    step_number,
):
    local_x, local_y, extent_z = checkpoint.shape
    grid_x = local_x * lax.axis_size("gx")
    grid_y = local_y * lax.axis_size("gy")
    place_x = lax.axis_index("gx")
    place_y = lax.axis_index("gy")
    anchor_x = place_x * local_x
    anchor_y = place_y * local_y
    clock = step_number.astype(jnp.float32)[0]
    rate_first = source_rate * (1.0 + 0.5 * jnp.sin(0.05 * clock))
    rate_second = source_rate * (1.0 + 0.5 * jnp.sin(0.05 * (clock + 1.0)))

    def masks(rim_width):
        return (
            validity(local_x, rim_width, place_x, grid_x),
            validity(local_y, rim_width, place_y, grid_y),
        )

    def sources(rates, rim_width):
        extent_x = local_x + 2 * rim_width
        extent_y = local_y + 2 * rim_width
        spot_x, spot_y, spot_z, inside = locate(
            source_cells,
            anchor_x - rim_width,
            anchor_y - rim_width,
            extent_x,
            extent_y,
            grid_y,
            extent_z,
        )
        blank = jnp.zeros((extent_x, extent_y, extent_z), jnp.float32)
        return blank.at[spot_x, spot_y, spot_z].add(rates * inside)

    stacked = jnp.stack((checkpoint, log_cond))
    padded = extended(stacked, (("gx", 1), ("gy", 2)), 3)
    state_zero = padded[0]
    cond_pad = padded[1]
    mask_x3, mask_y3 = masks(3)
    state_one = forward_step(state_zero, cond_pad, mask_x3, mask_y3, sources(rate_first, 3))
    mask_x2, mask_y2 = masks(2)
    cond_two = cond_pad[1:-1, 1:-1]
    final_wide = forward_step(state_one, cond_two, mask_x2, mask_y2, sources(rate_second, 2))
    final = final_wide[1:-1, 1:-1]
    missed = final - survey
    seed = survey_weight * missed
    spot_x, spot_y, spot_z, owned = locate(
        well_cells, anchor_x, anchor_y, local_x, local_y, grid_y, extent_z
    )
    nearby = final[spot_x, spot_y, spot_z] - well_data
    seed = seed.at[spot_x, spot_y, spot_z].add(well_weight * nearby * owned)
    partial_value = jnp.sum(survey_weight * missed * missed) + jnp.sum(
        owned * well_weight * nearby * nearby
    )
    seed, partial_value = (seed, partial_value)
    seed_pad = extended(seed, (("gx", 0), ("gy", 1)), 2)
    adjoint_one, sens_wide = adjoint_step(seed_pad, state_one, cond_two, mask_x2, mask_y2)
    sens_one = sens_wide[1:-1, 1:-1]
    mask_x1, mask_y1 = masks(1)
    adjoint_zero, sens_zero = adjoint_step(
        adjoint_one, state_zero[2:-2, 2:-2], cond_pad[2:-2, 2:-2], mask_x1, mask_y1
    )
    total = lax.psum(partial_value, ("gx", "gy"))
    misfit = (0.5 * total / (grid_x * grid_y * extent_z)).reshape(1)
    return (sens_one + sens_zero, adjoint_zero, final, misfit)


def solution(mesh):
    return jax.shard_map(
        on_device,
        mesh=mesh,
        in_specs=(
            P(("ens", "gx"), "gy", None),
            P(("ens", "gx"), "gy", None),
            P(("ens", "gx"), "gy", None),
            P(("ens", "gx"), "gy", None),
            P("ens"),
            P("ens"),
            P("ens"),
            P("ens"),
            P("ens"),
            P("ens"),
        ),
        out_specs=(
            P(("ens", "gx"), "gy", None),
            P(("ens", "gx"), "gy", None),
            P(("ens", "gx"), "gy", None),
            P("ens"),
        ),
        check_vma=False,
    )
```

profile of v0, /device:TPU:0, one launch (start us, length us, event | category | flops | bytes accessed | tf_op | source)
XLA Modules:
  0.0 141.6 jit_solution(17709376463260439989)
XLA Ops:
  0.7 1.3 pad_maximum_fusion.3
  2.0 1.3 collective-permute-start.1
  3.3 5.6 %collective-permute-start = (f32[2,3,128,128]{3,2,1,0:T(8,128)S(1)}, f32[2,3,128,128]{3,2,1,0:T(8,128)S(1)}, u32[]{:S(2)}, u32[]{:S(2)}) collective-permute-start(f32[2,3,128,128]{3,2,1,0:T(8,128)S(1)} %get-tuple-element.47), channel_id=1, source_target_pairs={{0,4},{4,8},{8,12},{1,5},{5,9},{9,13},{2,6},{6,10},{10,14},{3,7},{... | collective-permute-start | bytes 1179656 | tf_op jit(solution)/shard_map/ppermute | solution.py:17
  12.9 3.1 %collective-permute-done.1 = f32[2,3,128,128]{3,2,1,0:T(8,128)S(1)} collective-permute-done((f32[2,3,128,128]{3,2,1,0:T(8,128)S(1)}, f32[2,3,128,128]{3,2,1,0:T(8,128)S(1)}, u32[]{:S(2)}, u32[]{:S(2)}) %collective-permute-start.1) | collective-permute-done | bytes 393248 | tf_op jit(solution)/shard_map/ppermute | solution.py:20
  16.1 1.2 collective-permute-done
  17.3 1.3 collective-permute-start.3
  18.6 3.0 %collective-permute-start.2 = (f32[2,14,3,128]{3,2,1,0:T(4,128)S(1)}, f32[2,14,3,128]{3,2,1,0:T(4,128)S(1)}, u32[]{:S(2)}, u32[]{:S(2)}) collective-permute-start(f32[2,14,3,128]{3,2,1,0:T(4,128)S(1)} %get-tuple-element.39), channel_id=1, source_target_pairs={{0,1},{1,2},{2,3},{4,5},{5,6},{6,7},{8,9},{9,10},{10,11},{12,13},{... | collective-permute-start | bytes 129032 | tf_op jit(solution)/shard_map/ppermute | solution.py:17
  21.8 4.5 %scatter_fusion.1 = f32[12,132,128]{2,1,0:T(8,128)S(1)} fusion(f32[12,132,128]{2,1,0:T(8,128)S(1)} %broadcast_in_dim.46, s32[64]{0:T(128)S(1)} %get-tuple-element.97, f32[64]{0:T(128)S(1)} %and_select_fusion.4), kind=kCustom, calls=%fused_computation.2 | custom fusion | flops 64 | bytes 1536 | tf_op jit(solution)/shard_map/scatter-add | solution.py:142
  26.4 4.5 %scatter_fusion = f32[14,134,128]{2,1,0:T(8,128)S(1)} fusion(f32[14,134,128]{2,1,0:T(8,128)S(1)} %broadcast_in_dim.20, s32[64]{0:T(128)S(1)} %get-tuple-element.98, f32[64]{0:T(128)S(1)} %get-tuple-element.34), kind=kCustom, calls=%fused_computation.1 | custom fusion | flops 64 | bytes 1536 | tf_op jit(solution)/shard_map/scatter-add | solution.py:142
  31.8 1.2 pad_maximum_fusion
  33.2 1.1 broadcast_multiply_fusion
  36.3 1.1 copy-done.3
  38.1 1.4 %negate_multiply_fusion.1 = (f32[12,132,127]{2,1,0:T(8,128)S(1)}, f32[12,132,127]{2,1,0:T(8,128)}) fusion(f32[12,132,128]{2,1,0:T(8,128)S(1)} %fusion.25, f32[14,134,128]{2,1,0:T(8,128)S(1)} %get-tuple-element.37), kind=kLoop, calls=%fused_computation.69 | loop fusion | flops 1408176 | bytes 4828032 | tf_op jit(solution)/shard_map/mul | solution.py:46
  39.9 1.4 multiply_multiply_fusion.2
  42.6 1.3 fusion.103
  44.7 7.8 %gather_fusion = f32[256]{0:T(256)S(1)} fusion(f32[8,128,128]{2,1,0:T(8,128)} %get-tuple-element.29, s32[256]{0:T(256)S(1)} %bitcast.53), kind=kCustom, calls=%fused_computation | custom fusion | bytes 5120 | tf_op jit(solution)/shard_map/gather | solution.py:159
  53.2 15.3 %scatter_fusion.2 = f32[8,128,128]{2,1,0:T(8,128)S(1)} fusion(f32[8,128,128]{2,1,0:T(8,128)S(1)} %get-tuple-element.5, s32[256]{0:T(256)S(1)} %bitcast.52, f32[256]{0:T(256)S(1)} %get-tuple-element.96), kind=kCustom, calls=%fused_computation.3 | custom fusion | flops 256 | bytes 6144 | tf_op jit(solution)/shard_map/scatter-add | solution.py:160
  69.2 3.8 %collective-permute-start.4 = (f32[2,128,128]{2,1,0:T(8,128)}, f32[2,128,128]{2,1,0:T(8,128)S(1)}, u32[]{:S(2)}, u32[]{:S(2)}) collective-permute-start(f32[2,128,128]{2,1,0:T(8,128)} %get-tuple-element.94), channel_id=1, source_target_pairs={{0,4},{4,8},{8,12},{1,5},{5,9},{9,13},{2,6},{6,10},{10,14},{3,7},{... | collective-permute-start | bytes 393224 | tf_op jit(solution)/shard_map/ppermute | solution.py:17
  73.0 2.7 %fusion.110 = (f32[12,130,128]{2,1,0:T(8,128)}, f32[12,130,128]{2,1,0:T(8,128)}) fusion(f32[12,131,128]{2,1,0:T(8,128)} %get-tuple-element.31), kind=kLoop, calls=%fused_computation.265 | loop fusion | bytes 3194880 | tf_op jit(solution)/shard_map/slice | solution.py:82
  75.7 1.3 multiply_add_fusion.5
  77.0 1.3 collective-permute-start.5
  79.7 4.6 %collective-permute-done.5 = f32[2,128,128]{2,1,0:T(8,128)} collective-permute-done((f32[2,128,128]{2,1,0:T(8,128)}, f32[2,128,128]{2,1,0:T(8,128)}, u32[]{:S(2)}, u32[]{:S(2)}) %collective-permute-start.5) | collective-permute-done | bytes 131104 | tf_op jit(solution)/shard_map/ppermute | solution.py:20
  86.1 1.3 collective-permute-start.7
  87.4 3.0 %collective-permute-start.6 = (f32[12,2,128]{2,1,0:T(2,128)S(1)}, f32[12,2,128]{2,1,0:T(2,128)S(1)}, u32[]{:S(2)}, u32[]{:S(2)}) collective-permute-start(f32[12,2,128]{2,1,0:T(2,128)S(1)} %get-tuple-element.68), channel_id=1, source_target_pairs={{0,1},{1,2},{2,3},{4,5},{5,6},{6,7},{8,9},{9,10},{10,11},{12,13},{... | collective-permute-start | bytes 36872 | tf_op jit(solution)/shard_map/ppermute | solution.py:17
  90.5 1.1 fusion.120
  91.6 31.0 %psum.7 = f32[]{:T(128)} all-reduce(f32[]{:T(128)S(6)} %add.393), channel_id=1, replica_groups=mesh['ens'=2,'gx'=4,'gy'=4] {'gx','gy'}, use_global_device_ids=true, to_apply=%region_5.6 | all-reduce | flops 1 | bytes 8 | tf_op jit(solution)/shard_map/psum | solution.py:172
  122.6 2.0 %slice.680 = f32[10,132,128]{2,1,0:T(8,128)} slice(f32[11,132,128]{2,1,0:T(8,128)} %get-tuple-element.16), slice={[1:11], [0:132], [0:128]} | slice | bytes 1351680 | tf_op jit(solution)/shard_map/slice | solution.py:81
  126.1 1.3 pad_maximum_fusion.1
  129.1 1.0 copy-done.1
  130.7 1.0 copy-done.9
  137.4 1.5 %fusion.62 = f32[8,128,128]{2,1,0:T(8,128)} fusion(f32[10,130,128]{2,1,0:T(8,128)S(1)} %pad_slice_fusion.10, f32[10,130,128]{2,1,0:T(8,128)S(1)} %pad_slice_fusion.11, f32[10,128,128]{2,1,0:T(8,128)S(1)} %get-tuple-element.82, f32[10,128,128]{2,1,0:T(8,128)S(1)} %get-tuple-element.81, f32[10,128,128]{2,1,0:T(8,128)S(1)} %get-tuple-element.80, ...), kind=kLoop, calls=%fused_computation.133 | loop fusion | flops 1835008 | bytes 6815744 | tf_op jit(solution)/shard_map/add | solution.py:84
  138.9 1.6 %fusion.68 = f32[8,128,128]{2,1,0:T(8,128)} fusion(f32[10,130,128]{2,1,0:T(8,128)S(1)} %get-tuple-element.86, f32[10,130,128]{2,1,0:T(8,128)S(1)} %get-tuple-element.85, f32[10,128,128]{2,1,0:T(8,128)S(1)} %get-tuple-element.84, f32[10,128,128]{2,1,0:T(8,128)S(1)} %get-tuple-element.83, f32[8,130,128]{2,1,0:T(8,128)S(1)} %get-tuple-element.92, ...), kind=kLoop, calls=%fused_computation.148 | loop fusion | flops 1441792 | bytes 6815744 | tf_op jit(solution)/shard_map/add | solution.py:174
  (112 shorter events, 21.6 us)
Async XLA Ops:
  0.6 16.6 %copy-start.6 = (f32[8,128,128]{2,1,0:T(8,128)S(1)}, f32[8,128,128]{2,1,0:T(8,128)}, u32[]{:S(2)}) copy-start(f32[8,128,128]{2,1,0:T(8,128)} %param.10) | copy-start | bytes 1572868
  0.6 16.6 %copy-start.7 = (f32[8,128,128]{2,1,0:T(8,128)S(1)}, f32[8,128,128]{2,1,0:T(8,128)}, u32[]{:S(2)}) copy-start(f32[8,128,128]{2,1,0:T(8,128)} %param.11) | copy-start | bytes 1572868
  2.0 14.1 %collective-permute-start.1 = (f32[2,3,128,128]{3,2,1,0:T(8,128)S(1)}, f32[2,3,128,128]{3,2,1,0:T(8,128)S(1)}, u32[]{:S(2)}, u32[]{:S(2)}) collective-permute-start(f32[2,3,128,128]{3,2,1,0:T(8,128)S(1)} %get-tuple-element.48), channel_id=1, source_target_pairs={{4,0},{8,4},{12,8},{5,1},{9,5},{13,9},{6,2},{10,6},{14,10},{7,3},{... | collective-permute-start | bytes 1179656 | tf_op jit(solution)/shard_map/ppermute | solution.py:20
  3.3 13.9 %collective-permute-start = (f32[2,3,128,128]{3,2,1,0:T(8,128)S(1)}, f32[2,3,128,128]{3,2,1,0:T(8,128)S(1)}, u32[]{:S(2)}, u32[]{:S(2)}) collective-permute-start(f32[2,3,128,128]{3,2,1,0:T(8,128)S(1)} %get-tuple-element.47), channel_id=1, source_target_pairs={{0,4},{4,8},{8,12},{1,5},{5,9},{9,13},{2,6},{6,10},{10,14},{3,7},{... | collective-permute-start | bytes 1179656 | tf_op jit(solution)/shard_map/ppermute | solution.py:17
  17.3 4.4 %copy-start.15 = (f32[2,3,128,128]{3,2,1,0:T(8,128)}, f32[2,3,128,128]{3,2,1,0:T(8,128)S(1)}, u32[]{:S(2)}) copy-start(f32[2,3,128,128]{3,2,1,0:T(8,128)S(1)} %collective-permute-done) | copy-start | bytes 1179652
  17.3 13.6 %collective-permute-start.3 = (f32[2,14,3,128]{3,2,1,0:T(4,128)S(1)}, f32[2,14,3,128]{3,2,1,0:T(4,128)S(1)}, u32[]{:S(2)}, u32[]{:S(2)}) collective-permute-start(f32[2,14,3,128]{3,2,1,0:T(4,128)S(1)} %get-tuple-element.40), channel_id=1, source_target_pairs={{1,0},{2,1},{3,2},{5,4},{6,5},{7,6},{9,8},{10,9},{11,10},{13,12},{... | collective-permute-start | bytes 129032 | tf_op jit(solution)/shard_map/ppermute | solution.py:20
  18.6 12.3 %collective-permute-start.2 = (f32[2,14,3,128]{3,2,1,0:T(4,128)S(1)}, f32[2,14,3,128]{3,2,1,0:T(4,128)S(1)}, u32[]{:S(2)}, u32[]{:S(2)}) collective-permute-start(f32[2,14,3,128]{3,2,1,0:T(4,128)S(1)} %get-tuple-element.39), channel_id=1, source_target_pairs={{0,1},{1,2},{2,3},{4,5},{5,6},{6,7},{8,9},{9,10},{10,11},{12,13},{... | collective-permute-start | bytes 129032 | tf_op jit(solution)/shard_map/ppermute | solution.py:17
  30.9 0.9 copy-start.2
  34.2 7.1 %copy-start = (f32[11,132,128]{2,1,0:T(8,128)}, f32[11,132,128]{2,1,0:T(8,128)S(1)}, u32[]{:S(2)}) copy-start(f32[11,132,128]{2,1,0:T(8,128)S(1)} %get-tuple-element.17) | copy-start | bytes 2230276
  36.2 1.2 copy-start.3
  41.6 1.0 copy-start.18
  42.6 1.4 copy-start.17
  44.0 8.5 %copy-start.19 = (f32[256]{0:T(256)S(1)}, f32[256]{0:T(256)}, u32[]{:S(2)}) copy-start(f32[256]{0:T(256)} %param.16) | copy-start | bytes 3076
  44.0 8.5 %copy-start.20 = (f32[256]{0:T(256)S(1)}, f32[256]{0:T(256)}, u32[]{:S(2)}) copy-start(f32[256]{0:T(256)} %param.15) | copy-start | bytes 3076
  69.2 10.4 %collective-permute-start.4 = (f32[2,128,128]{2,1,0:T(8,128)}, f32[2,128,128]{2,1,0:T(8,128)S(1)}, u32[]{:S(2)}, u32[]{:S(2)}) collective-permute-start(f32[2,128,128]{2,1,0:T(8,128)} %get-tuple-element.94), channel_id=1, source_target_pairs={{0,4},{4,8},{8,12},{1,5},{5,9},{9,13},{2,6},{6,10},{10,14},{3,7},{... | collective-permute-start | bytes 393224 | tf_op jit(solution)/shard_map/ppermute | solution.py:17
  77.0 7.3 %collective-permute-start.5 = (f32[2,128,128]{2,1,0:T(8,128)}, f32[2,128,128]{2,1,0:T(8,128)}, u32[]{:S(2)}, u32[]{:S(2)}) collective-permute-start(f32[2,128,128]{2,1,0:T(8,128)} %get-tuple-element.93), channel_id=1, source_target_pairs={{4,0},{8,4},{12,8},{5,1},{9,5},{13,9},{6,2},{10,6},{14,10},{7,3},{... | collective-permute-start | bytes 393224 | tf_op jit(solution)/shard_map/ppermute | solution.py:20
  79.6 10.9 %copy-start.5 = (f32[9,130,128]{2,1,0:T(8,128)S(1)}, f32[9,130,128]{2,1,0:T(8,128)}, u32[]{:S(2)}) copy-start(f32[9,130,128]{2,1,0:T(8,128)} %get-tuple-element.6) | copy-start | bytes 1797124
  79.7 44.9 %copy-start.4 = (f32[9,130,128]{2,1,0:T(8,128)S(1)}, f32[9,130,128]{2,1,0:T(8,128)}, u32[]{:S(2)}) copy-start(f32[9,130,128]{2,1,0:T(8,128)} %get-tuple-element.7) | copy-start | bytes 1797124
  85.2 0.9 copy-start.16
  86.1 40.0 %collective-permute-start.7 = (f32[12,2,128]{2,1,0:T(2,128)S(1)}, f32[12,2,128]{2,1,0:T(2,128)S(1)}, u32[]{:S(2)}, u32[]{:S(2)}) collective-permute-start(f32[12,2,128]{2,1,0:T(2,128)S(1)} %get-tuple-element.69), channel_id=1, source_target_pairs={{1,0},{2,1},{3,2},{5,4},{6,5},{7,6},{9,8},{10,9},{11,10},{13,12},{... | collective-permute-start | bytes 36872 | tf_op jit(solution)/shard_map/ppermute | solution.py:20
  87.4 38.7 %collective-permute-start.6 = (f32[12,2,128]{2,1,0:T(2,128)S(1)}, f32[12,2,128]{2,1,0:T(2,128)S(1)}, u32[]{:S(2)}, u32[]{:S(2)}) collective-permute-start(f32[12,2,128]{2,1,0:T(2,128)S(1)} %get-tuple-element.68), channel_id=1, source_target_pairs={{0,1},{1,2},{2,3},{4,5},{5,6},{6,7},{8,9},{9,10},{10,11},{12,13},{... | collective-permute-start | bytes 36872 | tf_op jit(solution)/shard_map/ppermute | solution.py:17
  126.1 1.4 copy-start.8
  129.0 1.1 copy-start.1
  130.5 1.2 copy-start.9
  130.5 1.4 copy-start.10
  130.6 1.6 %copy-start.11 = (f32[10,132,128]{2,1,0:T(8,128)S(1)}, f32[10,132,128]{2,1,0:T(8,128)}, u32[]{:S(2)}) copy-start(f32[10,132,128]{2,1,0:T(8,128)} %slice.680) | copy-start | bytes 2027524
  136.0 1.1 copy-start.12
  136.1 1.2 copy-start.13
  136.1 1.4 copy-start.14
where the time goes:
time: 143 us; the launch traced here: 142 us
  other arithmetic  48.5 us (34%)
  blocking collectives  31 us (22%)
  local copies, waits for them, and re-layouts  27.4 us (19%)
  starting transfers between devices  20.6 us (14%)
  waiting for transfers between devices  8.95 us (6%)
  between operations  5.14 us (4%)
    psum x1, blocking collectives, on_device(): total = lax.psum(partial_value, ('gx', 'gy'))  31 us
    ppermute x4, starting transfers between devices, extended(): lax.ppermute(lax.slice_in_dim(block, block.shape[dim] - width, None, axis...  15.5 us
    scatter-add x1, other arithmetic, on_device(): seed = seed.at[spot_x, spot_y, spot_z].add(well_weight * nearby * owned)  15.3 us
    scatter-add x2, other arithmetic, sources(): return blank.at[spot_x, spot_y, spot_z].add(rates * inside)  8.99 us
    gather x1, local copies, waits for them, and re-layouts, on_device(): nearby = final[spot_x, spot_y, spot_z] - well_data  7.79 us
    ppermute x4, waiting for transfers between devices, extended(): lax.ppermute(lax.slice_in_dim(block, 0, width, axis=dim), axis, backward)  7.76 us
    unnamed x44, local copies, waits for them, and re-layouts  7.52 us
    ppermute x4, starting transfers between devices, extended(): lax.ppermute(lax.slice_in_dim(block, 0, width, axis=dim), axis, backward)  5.16 us
  transfers between devices with their start and end apart: 8, of which 3 were waited for; matrix products, arithmetic and copies ran while one was open for 14% of the time, Pallas kernels for 0%

commit v1 on v0

v1 whole, which is shorter than its diff:
```python
import functools

import jax
import jax.numpy as jnp
from jax import lax
from jax.experimental import pallas as pl
from jax.experimental.pallas import tpu as pltpu
from jax.sharding import PartitionSpec as P

time_step = 0.2
head_slope = 0.5
molecular = 0.05
dispersivity = 0.1

RIM = 2
PAD = 8
DIRS = ((1, 0), (-1, 0), (0, 1), (0, -1), (1, 1), (1, -1), (-1, 1), (-1, -1))
MESH = pl.DeviceIdType.MESH


def split3(values):
    high = values.astype(jnp.bfloat16)
    rest = values - high.astype(jnp.float32)
    mid = rest.astype(jnp.bfloat16)
    low = (rest - mid.astype(jnp.float32)).astype(jnp.bfloat16)
    return high, mid, low


def dot_t(a, b):
    return lax.dot_general(a, b, (((1,), (1,)), ((), ())), preferred_element_type=jnp.float32)


def up_y(v):
    return pltpu.roll(v, v.shape[0] - 1, 0)


def down_y(v):
    return pltpu.roll(v, 1, 0)


def up_z(v):
    return pltpu.roll(v, v.shape[1] - 1, 1)


def down_z(v):
    return pltpu.roll(v, 1, 1)


def source_slices(dx, dy, lx, ly):
    width = RIM if dy == 0 else 1
    if dx == 0:
        xs, xd = (0, lx), RIM
    elif dx > 0:
        xs, xd = (lx - width, width), RIM - width
    else:
        xs, xd = (0, width), lx + RIM
    if dy == 0:
        ys, yd = (0, ly), PAD
    elif dy > 0:
        ys, yd = (ly - PAD, PAD), 0
    else:
        ys, yd = (0, PAD), ly + PAD
    return xs, ys, xd, yd


def kernel(
    nx,
    ny,
    lc_ref,
    c_ref,
    survey_ref,
    weight_ref,
    wcell_ref,
    wdata_ref,
    wweight_ref,
    scell_ref,
    srate_ref,
    step_ref,
    grad_ref,
    adj_ref,
    conc_ref,
    misfit_ref,
    h,
    c0,
    c1,
    a2,
    a1,
    fu,
    fl,
    ky,
    kz,
    q,
    ww,
    wd,
    sv,
    sw,
    red_y,
    red_x,
    local_sem,
    send1,
    recv1,
    send2,
    recv2,
    send_y,
    recv_y,
    send_x,
    recv_x,
):
    f32 = jnp.float32
    lx, ly, nz = c_ref.shape
    rows = ly + 2 * PAD
    i = lax.axis_index("gx")
    j = lax.axis_index("gy")
    body = (slice(None), pl.ds(PAD, ly), slice(None))

    loads = [
        pltpu.make_async_copy(lc_ref, h.at[pl.ds(RIM, lx), pl.ds(PAD, ly)], local_sem.at[0]),
        pltpu.make_async_copy(c_ref, c0.at[pl.ds(RIM, lx), pl.ds(PAD, ly)], local_sem.at[1]),
        pltpu.make_async_copy(survey_ref, sv, local_sem.at[2]),
        pltpu.make_async_copy(weight_ref, sw, local_sem.at[3]),
    ]

    def inside(a, b):
        return (a >= 0) & (a < nx) & (b >= 0) & (b < ny)

    barrier = pltpu.get_barrier_semaphore()

    def greet(di, dj):
        pl.semaphore_signal(barrier, inc=1, device_id={"gx": di, "gy": dj}, device_id_type=MESH)

    for dx, dy in DIRS[4:]:

        @pl.when(inside(i + dx, j + dy))
        def _():
            greet(i + dx, j + dy)

    @pl.loop(1, nx)
    def _(o):
        greet(lax.rem(i + o, nx), j)

    @pl.loop(1, ny)
    def _(o):
        greet(i, lax.rem(j + o, ny))

    for load in loads:
        load.start()

    def one(flag):
        return jnp.where(flag, 1, 0)

    sides = (one(i > 0) + one(i < nx - 1)) * (one(j > 0) + one(j < ny - 1))
    pl.semaphore_wait(barrier, nx - 1 + ny - 1 + sides)

    def remote(d, src, dst, off_x, off_y, send, recv):
        dx, dy = DIRS[d]
        xs, ys, xd, yd = source_slices(dx, dy, lx, ly)
        return pltpu.make_async_remote_copy(
            src_ref=src.at[pl.ds(xs[0] + off_x, xs[1]), pl.ds(ys[0] + off_y, ys[1])],
            dst_ref=dst.at[pl.ds(xd, xs[1]), pl.ds(yd, ys[1])],
            send_sem=send,
            recv_sem=recv,
            device_id={"gx": i + dx, "gy": j + dy},
            device_id_type=MESH,
        )

    first = [
        [
            remote(d, c_ref, c0, 0, 0, send1.at[2 * d], recv1.at[2 * d]),
            remote(d, lc_ref, h, 0, 0, send1.at[2 * d + 1], recv1.at[2 * d + 1]),
        ]
        for d in range(8)
    ]
    second = [[remote(d, a2, a2, RIM, PAD, send2.at[d], recv2.at[d])] for d in range(8)]

    def start(copies, d):
        dx, dy = DIRS[d]

        @pl.when(inside(i + dx, j + dy))
        def _():
            for copy in copies[d]:
                copy.start()

    def arrive(copies, d):
        dx, dy = DIRS[d]

        @pl.when(inside(i - dx, j - dy))
        def _():
            for copy in copies[d]:
                copy.wait_recv()

    def sent(copies, d):
        dx, dy = DIRS[d]

        @pl.when(inside(i + dx, j + dy))
        def _():
            for copy in copies[d]:
                copy.wait_send()

    for d in (2, 3, 4, 5, 6, 7, 0, 1):
        start(first, d)

    def fill(d, refs):
        dx, dy = DIRS[d]
        xs, ys, xd, yd = source_slices(dx, dy, lx, ly)

        @pl.when(jnp.logical_not(inside(i - dx, j - dy)))
        def _():
            for ref in refs:
                ref[pl.ds(xd, xs[1]), pl.ds(yd, ys[1])] = jnp.zeros((xs[1], ys[1], nz), f32)

    for d in range(8):
        fill(d, (c0, h, a2))
    for ref in (c0, h, a2):
        for x in (0, lx + 2 * RIM - 1):
            for y in (0, ly + PAD):
                ref[x, pl.ds(y, PAD)] = jnp.zeros((PAD, nz), f32)

    grid_y = ly * ny
    wcell = wcell_ref[...].reshape(1, -1)
    scell = scell_ref[...].reshape(1, -1)
    wweight = wweight_ref[...].reshape(1, -1)
    wdata = wdata_ref[...].reshape(1, -1)
    srate = srate_ref[...].reshape(1, -1)
    nobs, nsrc = wcell.shape[1], scell.shape[1]
    zi = lax.broadcasted_iota(jnp.int32, (nz, nobs), 0)
    at_z = zi == lax.rem(wcell, nz)
    well_parts = []
    for part_w, part_d in zip(split3(wweight), split3(wweight * wdata)):
        both = [jnp.where(at_z, p.astype(f32), 0.0).astype(jnp.bfloat16) for p in (part_w, part_d)]
        well_parts.append(jnp.concatenate(both, axis=0))
    src_z = lax.broadcasted_iota(jnp.int32, (nz, nsrc), 0) == lax.rem(scell, nz)
    src_parts = [jnp.where(src_z, p.astype(f32), 0.0).astype(jnp.bfloat16) for p in split3(srate)]
    src_parts = jnp.concatenate(src_parts, axis=0)
    well_row = lax.div(wcell, nz) - (i * lx * grid_y + j * ly)
    src_row = lax.div(scell, nz) - (i * lx * grid_y + j * ly)
    well_iota = lax.broadcasted_iota(jnp.int32, (ly, nobs), 0)
    src_iota = lax.broadcasted_iota(jnp.int32, (rows, nsrc), 0) - PAD

    @pl.loop(0, lx)
    def _(x):
        hot = jnp.where(well_iota == well_row - x * grid_y, 1.0, 0.0).astype(jnp.bfloat16)
        both = dot_t(hot, well_parts[0]) + dot_t(hot, well_parts[1]) + dot_t(hot, well_parts[2])
        ww[x] = both[:, :nz]
        wd[x] = both[:, nz:]

    @pl.loop(0, lx + 2)
    def _(x):
        hot = jnp.where(src_iota == src_row - (x - 1) * grid_y, 1.0, 0.0).astype(jnp.bfloat16)
        parts = dot_t(hot, src_parts)
        q[x] = parts[:, :nz] + parts[:, nz : 2 * nz] + parts[:, 2 * nz :]

    clock = jnp.full((1, nz), step_ref[0], jnp.int32).astype(f32)
    gain_first = time_step * (1.0 + 0.5 * jnp.sin(0.05 * clock))
    gain_second = time_step * (1.0 + 0.5 * jnp.sin(0.05 * (clock + 1.0)))

    lane = lax.broadcasted_iota(jnp.int32, (rows, nz), 1)
    row = lax.broadcasted_iota(jnp.int32, (rows, nz), 0)
    low_face = jnp.where(j == 0, PAD - 1, -1)
    high_face = jnp.where(j == ny - 1, PAD + ly - 1, -1)

    def faces_in(x):
        open_z = lane < nz - 1
        open_y = (row != low_face) & (row != high_face)
        half = h[x]
        ky[x] = jnp.where(
            open_y, time_step * molecular + time_step * dispersivity * (half * up_y(half)), 0.0
        )
        kz[x] = jnp.where(
            open_z, time_step * molecular + time_step * dispersivity * (half * up_z(half)), 0.0
        )

    def root(x):
        h[x] = jnp.exp(0.5 * h[x])

    def faces_x(x):
        cond = time_step * (h[x] * h[x + 1])
        closed = ((i == 0) & (x == RIM - 1)) | ((i == nx - 1) & (x == RIM + lx - 1))
        keep = jnp.where(closed, 0.0, 1.0)
        fu[x] = keep * (time_step * molecular + (head_slope + dispersivity) * cond)
        fl[x] = keep * (time_step * molecular + dispersivity * cond)

    def spread_yz(v, x):
        gy = ky[x] * (up_y(v) - v)
        gz = kz[x] * (up_z(v) - v)
        return (gy - down_y(gy)) + (gz - down_z(gz))

    def forward(src, x):
        v = src[x]
        out = fu[x] * v - fl[x] * src[x + 1]
        into = fu[x - 1] * src[x - 1] - fl[x - 1] * v
        return v + ((into - out) + spread_yz(v, x))

    def backward(src, x):
        v = src[x]
        above = src[x + 1] - v
        below = v - src[x - 1]
        return v + ((above * fu[x] - below * fl[x - 1]) + spread_yz(v, x))

    def do_c1(x):
        c1[x] = forward(c0, x) + gain_first * q[x - 1]

    def do_c2(x, total):
        final = (forward(c1, x) + gain_second * q[x - 1])[PAD : PAD + ly]
        b = x - RIM
        conc_ref[b] = final
        missed = final - sv[b]
        seed = sw[b] * missed
        heavy = ww[b] * final
        pulled = wd[b]
        a2[x, pl.ds(PAD, ly)] = seed + (heavy - pulled)
        term = seed * missed + final * (heavy - 2.0 * pulled)
        return total + jnp.sum(term.reshape(ly // 8, 8, nz), axis=0)

    def do_a1(x):
        a1[x] = backward(a2, x)

    def do_out(x):
        b = x - RIM
        v1, v2 = a1[x], a2[x]
        t0, t1 = c0[x], c1[x]
        lean = (head_slope + dispersivity)

        def face_x(p):
            low1 = lean * c1[p] - dispersivity * c1[p + 1]
            low0 = lean * c0[p] - dispersivity * c0[p + 1]
            d1 = a1[p + 1] - a1[p]
            d2 = a2[p + 1] - a2[p]
            return (fu[p] - fl[p]) * (d2 * low1 + d1 * low0), d1

        gx_up, above = face_x(x)
        gx_low, below = face_x(x - 1)
        grad = gx_up + gx_low
        new = v1 + (above * fu[x] - below * fl[x - 1])
        for k, up, down in ((ky[x], up_y, down_y), (kz[x], up_z, down_z)):
            d1 = up(v1) - v1
            flow = k * d1
            new = new + (flow - down(flow))
            sens = (d1 * (up(t0) - t0) + (up(v2) - v2) * (up(t1) - t1)) * (
                -0.5 * jnp.maximum(k - time_step * molecular, 0.0)
            )
            grad = grad + (sens + down(sens))
        grad_ref[b] = grad[PAD : PAD + ly]
        adj_ref[b] = new[PAD : PAD + ly]

    def loop(low, high, f):
        @pl.loop(low, high)
        def _(x):
            f(x)

    lo, hi = RIM, RIM + lx
    for load in loads:
        load.wait()
    arrive(first, 2)
    arrive(first, 3)
    loop(lo, hi, root)
    loop(lo, hi, faces_in)
    loop(lo, hi - 1, faces_x)
    loop(lo + 1, hi - 1, do_c1)
    total = lax.fori_loop(lo + 2, hi - 2, do_c2, jnp.zeros((8, nz), f32))

    for d in (0, 1, 4, 5, 6, 7):
        arrive(first, d)
    for x in (lo - 2, lo - 1, hi, hi + 1):
        root(x)
    for x in (lo - 1, hi):
        faces_in(x)
    for x in (lo - 2, lo - 1, hi - 1, hi):
        faces_x(x)
    for x in (lo - 1, lo, hi - 1, hi):
        do_c1(x)
    for x in (lo, hi - 1, lo + 1, hi - 2):
        total = do_c2(x, total)

    for d in (0, 1, 2, 3, 4, 5, 6, 7):
        start(second, d)

    def reduce_start(ref, axis, me, count, send, recv):
        @pl.loop(1, count)
        def _(o):
            pltpu.make_async_remote_copy(
                src_ref=ref.at[me],
                dst_ref=ref.at[me],
                send_sem=send.at[o],
                recv_sem=recv.at[me],
                device_id={axis: lax.rem(me + o, count)},
                device_id_type=MESH,
            ).start()

    def reduce_wait(ref, axis, me, count, send, recv):
        @pl.loop(1, count)
        def _(o):
            other = lax.rem(me + o, count)
            copy = pltpu.make_async_remote_copy(
                src_ref=ref.at[me],
                dst_ref=ref.at[other],
                send_sem=send.at[o],
                recv_sem=recv.at[other],
                device_id={axis: other},
                device_id_type=MESH,
            )
            copy.wait_send()
            copy.wait_recv()

    red_y[j] = total
    reduce_start(red_y, "gy", j, ny, send_y, recv_y)

    for d in (2, 3):
        arrive(second, d)
    loop(lo + 2, hi - 2, do_a1)

    reduce_wait(red_y, "gy", j, ny, send_y, recv_y)
    red_x[i] = jnp.sum(red_y[...], axis=0)
    reduce_start(red_x, "gx", i, nx, send_x, recv_x)

    do_a1(lo + 1)
    do_a1(hi - 2)
    loop(lo + 2, hi - 2, do_out)

    for d in (0, 1, 4, 5, 6, 7):
        arrive(second, d)
    for x in (lo - 1, lo, hi - 1, hi):
        do_a1(x)
    for x in (lo, lo + 1, hi - 2, hi - 1):
        do_out(x)

    reduce_wait(red_x, "gx", i, nx, send_x, recv_x)
    wells = jnp.sum(wweight * wdata * wdata)
    whole = jnp.sum(jnp.sum(red_x[...], axis=0)) + wells
    misfit_ref[0] = whole * (0.5 / (nx * lx * grid_y * nz))
    for d in range(8):
        sent(first, d)
        sent(second, d)


def on_device(*args):
    lx, ly, nz = args[1].shape
    nx = lax.axis_size("gx")
    ny = lax.axis_size("gy")
    rows = ly + 2 * PAD
    wide = pltpu.VMEM((lx + 2 * RIM, rows, nz), jnp.float32)
    block = pltpu.VMEM((lx, ly, nz), jnp.float32)
    field = jax.ShapeDtypeStruct((lx, ly, nz), jnp.float32)
    anywhere = pl.BlockSpec(memory_space=pl.ANY)
    vmem = pl.BlockSpec(memory_space=pltpu.VMEM)
    smem = pl.BlockSpec(memory_space=pltpu.SMEM)
    dma = pltpu.SemaphoreType.DMA
    return pl.pallas_call(
        functools.partial(kernel, nx, ny),
        out_shape=(field, field, field, jax.ShapeDtypeStruct((1,), jnp.float32)),
        in_specs=[anywhere] * 4 + [vmem] * 5 + [smem],
        out_specs=(vmem, vmem, vmem, smem),
        scratch_shapes=[wide] * 9
        + [pltpu.VMEM((lx + 2, rows, nz), jnp.float32)]
        + [block] * 4
        + [pltpu.VMEM((ny, 8, nz), jnp.float32), pltpu.VMEM((nx, 8, nz), jnp.float32)]
        + [dma((4,)), dma((16,)), dma((16,)), dma((8,)), dma((8,))]
        + [dma((ny,)), dma((ny,)), dma((nx,)), dma((nx,))],
        compiler_params=pltpu.CompilerParams(
            collective_id=0, has_side_effects=True, vmem_limit_bytes=40 * 1024 * 1024
        ),
    )(*args)


def solution(mesh):
    return jax.shard_map(
        on_device,
        mesh=mesh,
        in_specs=(P(("ens", "gx"), "gy", None),) * 4 + (P("ens"),) * 6,
        out_specs=(P(("ens", "gx"), "gy", None),) * 3 + (P("ens"),),
        check_vma=False,
    )
```

time: 143 us -> 33.1 us (0.23)
  other arithmetic: 48.5 us -> 0 us
  blocking collectives: 31 us -> 0 us
  Pallas kernels: 0 us -> 21.1 us
  starting transfers between devices: 20.6 us -> 0 us
  local copies, waits for them, and re-layouts: 27.4 us -> 8.56 us
  waiting for transfers between devices: 8.95 us -> 0 us
  between operations: 5.14 us -> 3.11 us
    psum x1 -> x0, blocking collectives: 31 us -> none  [on_device(): total = lax.psum(partial_value, ('gx', 'gy'))]
    scatter-add x3 -> x0, other arithmetic: 24.3 us -> none  [the longest x1 15.3 us: on_device(): seed = seed.at[spot_x, spot_y, spot_z].add(well_weight * nearby * owned)]
    pallas_call x0 -> x1, Pallas kernels: none -> 21.1 us  [on_device(): pl.pallas_call(functools.partial(kernel, nx, ny), out_shape=(field, field...]
    ppermute x8 -> x0, starting transfers between devices: 20.6 us -> none  [the longest x4 15.5 us: extended(): lax.ppermute(lax.slice_in_dim(block, block.shape[dim] - width, None, axis...]
    slice x33 -> x0, local copies, waits for them, and re-layouts: 10.9 us -> none  [the longest x4 4.07 us: adjoint_step(): push_x[1:] + pull_x[:-1]]
    mul x21 -> x0, other arithmetic: 10.4 us -> none  [the longest x2 2.05 us: forward_step(): -(molecular + dispersivity * cond_z)]
    ppermute x8 -> x0, waiting for transfers between devices: 8.95 us -> none  [the longest x4 7.76 us: extended(): lax.ppermute(lax.slice_in_dim(block, 0, width, axis=dim), axis, backward)]
    gather x1 -> x0, local copies, waits for them, and re-layouts: 7.79 us -> none  [on_device(): nearby = final[spot_x, spot_y, spot_z] - well_data]
  transfers between devices with their start and end apart: 8 -> 0, of which waited for: 3 -> 0; matrix products, arithmetic and copies ran while one was open for 14% -> 0% of each run, Pallas kernels for 0% -> 0%
where the time goes in v1:
time: 33.1 us; the launch traced here: 32.7 us
  Pallas kernels  21.1 us (64%)
  local copies, waits for them, and re-layouts  8.56 us (26%)
  between operations  3.11 us (9%)
    pallas_call x1, Pallas kernels, on_device(): pl.pallas_call(functools.partial(kernel, nx, ny), out_shape=(field, field...  21.1 us
    unnamed x21, local copies, waits for them, and re-layouts  8.56 us

profile of v1, /device:TPU:0, one launch (start us, length us, event | category | flops | bytes accessed | tf_op | source)
XLA Modules:
  0.0 32.7 jit_solution(15245164451610430944)
XLA Ops:
  0.6 0.0 copy-start.7
  0.6 0.0 copy-start.4
  1.3 0.0 copy-done.7
  1.3 0.0 copy-done.4
  1.3 0.0 copy-start
  1.3 1.0 %copy-done = f32[8,128,128]{2,1,0:T(8,128)S(1)} copy-done((f32[8,128,128]{2,1,0:T(8,128)S(1)}, f32[8,128,128]{2,1,0:T(8,128)}, u32[]{:S(2)}) %copy-start) | copy-done | bytes 524312
  2.4 0.0 copy-start.1
  2.4 1.0 %copy-done.1 = f32[8,128,128]{2,1,0:T(8,128)S(1)} copy-done((f32[8,128,128]{2,1,0:T(8,128)S(1)}, f32[8,128,128]{2,1,0:T(8,128)}, u32[]{:S(2)}) %copy-start.1) | copy-done | bytes 524312
  3.4 0.0 copy-start.2
  3.4 1.0 %copy-done.2 = f32[8,128,128]{2,1,0:T(8,128)S(1)} copy-done((f32[8,128,128]{2,1,0:T(8,128)S(1)}, f32[8,128,128]{2,1,0:T(8,128)}, u32[]{:S(2)}) %copy-start.2) | copy-done | bytes 524312
  4.5 0.0 copy-start.3
  4.5 1.0 %copy-done.3 = f32[8,128,128]{2,1,0:T(8,128)S(1)} copy-done((f32[8,128,128]{2,1,0:T(8,128)S(1)}, f32[8,128,128]{2,1,0:T(8,128)}, u32[]{:S(2)}) %copy-start.3) | copy-done | bytes 524312
  5.5 0.0 copy-start.5
  5.5 0.7 %copy-done.5 = f32[256]{0:T(256)S(1)} copy-done((f32[256]{0:T(256)S(1)}, f32[256]{0:T(256)}, u32[]{:S(2)}) %copy-start.5) | copy-done | bytes 1048
  6.2 0.0 copy-start.6
  6.2 0.7 %copy-done.6 = f32[256]{0:T(256)S(1)} copy-done((f32[256]{0:T(256)S(1)}, f32[256]{0:T(256)}, u32[]{:S(2)}) %copy-start.6) | copy-done | bytes 1048
  6.9 0.0 copy-start.8
  6.9 0.7 %copy-done.8 = f32[64]{0:T(128)S(1)} copy-done((f32[64]{0:T(128)S(1)}, f32[64]{0:T(128)}, u32[]{:S(2)}) %copy-start.8) | copy-done | bytes 280
  7.5 21.1 %shard_map.129 = (f32[8,128,128]{2,1,0:T(8,128)S(1)}, f32[8,128,128]{2,1,0:T(8,128)S(1)}, f32[8,128,128]{2,1,0:T(8,128)S(1)}, f32[1]{0:T(128)}) custom-call(f32[8,128,128]{2,1,0:T(8,128)S(1)} %copy-done, f32[8,128,128]{2,1,0:T(8,128)S(1)} %copy-done.1, f32[8,128,128]{2,1,0:T(8,128)S(1)} %copy-done.2, f32[8,128,128]{2,1,0:T(8,128)S(1)} %copy-done.3, ...), custom_call_target="tpu_custom_call" | custom-call | tf_op jit(solution)/shard_map/pallas_call | solution.py:447
  28.6 0.8 %copy.19 = f32[8,128,128]{2,1,0:T(8,128)} copy(f32[8,128,128]{2,1,0:T(8,128)S(1)} %get-tuple-element.8) | data formatting | bytes 1048576
  29.4 0.8 %copy.20 = f32[8,128,128]{2,1,0:T(8,128)} copy(f32[8,128,128]{2,1,0:T(8,128)S(1)} %get-tuple-element.9) | data formatting | bytes 1048576
  30.2 0.8 %copy.21 = f32[8,128,128]{2,1,0:T(8,128)} copy(f32[8,128,128]{2,1,0:T(8,128)S(1)} %get-tuple-element.10) | data formatting | bytes 1048576
Async XLA Ops:
  0.6 0.7 %copy-start.7 = (s32[64]{0:T(128)S(1)}, s32[64]{0:T(128)}, u32[]{:S(2)}) copy-start(s32[64]{0:T(128)} %scell_ref.1) | copy-start | bytes 772
  0.6 0.7 %copy-start.4 = (s32[256]{0:T(256)S(1)}, s32[256]{0:T(256)}, u32[]{:S(2)}) copy-start(s32[256]{0:T(256)} %wcell_ref.1) | copy-start | bytes 3076
  1.3 1.0 %copy-start = (f32[8,128,128]{2,1,0:T(8,128)S(1)}, f32[8,128,128]{2,1,0:T(8,128)}, u32[]{:S(2)}) copy-start(f32[8,128,128]{2,1,0:T(8,128)} %lc_ref.1) | copy-start | bytes 1572868
  2.4 1.0 %copy-start.1 = (f32[8,128,128]{2,1,0:T(8,128)S(1)}, f32[8,128,128]{2,1,0:T(8,128)}, u32[]{:S(2)}) copy-start(f32[8,128,128]{2,1,0:T(8,128)} %c_ref.1) | copy-start | bytes 1572868
  3.4 1.0 %copy-start.2 = (f32[8,128,128]{2,1,0:T(8,128)S(1)}, f32[8,128,128]{2,1,0:T(8,128)}, u32[]{:S(2)}) copy-start(f32[8,128,128]{2,1,0:T(8,128)} %survey_ref.1) | copy-start | bytes 1572868
  4.5 1.0 %copy-start.3 = (f32[8,128,128]{2,1,0:T(8,128)S(1)}, f32[8,128,128]{2,1,0:T(8,128)}, u32[]{:S(2)}) copy-start(f32[8,128,128]{2,1,0:T(8,128)} %weight_ref.1) | copy-start | bytes 1572868
  5.5 0.7 %copy-start.5 = (f32[256]{0:T(256)S(1)}, f32[256]{0:T(256)}, u32[]{:S(2)}) copy-start(f32[256]{0:T(256)} %wdata_ref.1) | copy-start | bytes 3076
  6.2 0.7 %copy-start.6 = (f32[256]{0:T(256)S(1)}, f32[256]{0:T(256)}, u32[]{:S(2)}) copy-start(f32[256]{0:T(256)} %wweight_ref.1) | copy-start | bytes 3076
  6.9 0.7 %copy-start.8 = (f32[64]{0:T(128)S(1)}, f32[64]{0:T(128)}, u32[]{:S(2)}) copy-start(f32[64]{0:T(128)} %srate_ref.1) | copy-start | bytes 772

commit v2 on v1

--- a/solution.py
+++ b/solution.py
@@ -70,11 +70,11 @@
     c_ref,
     survey_ref,
     weight_ref,
-    wcell_ref,
-    wdata_ref,
-    wweight_ref,
-    scell_ref,
-    srate_ref,
+    wcell_hbm,
+    wdata_hbm,
+    wweight_hbm,
+    scell_hbm,
+    srate_hbm,
     step_ref,
     grad_ref,
     adj_ref,
@@ -94,6 +94,11 @@
     wd,
     sv,
     sw,
+    wcell_ref,
+    wdata_ref,
+    wweight_ref,
+    scell_ref,
+    srate_ref,
     red_y,
     red_x,
     local_sem,
@@ -120,6 +125,19 @@
         pltpu.make_async_copy(weight_ref, sw, local_sem.at[3]),
     ]
 
+    small = [
+        pltpu.make_async_copy(src, dst, local_sem.at[4 + k])
+        for k, (src, dst) in enumerate(
+            (
+                (wcell_hbm, wcell_ref),
+                (wdata_hbm, wdata_ref),
+                (wweight_hbm, wweight_ref),
+                (scell_hbm, scell_ref),
+                (srate_hbm, srate_ref),
+            )
+        )
+    ]
+
     def inside(a, b):
         return (a >= 0) & (a < nx) & (b >= 0) & (b < ny)
 
@@ -142,7 +160,7 @@
     def _(o):
         greet(i, lax.rem(j + o, ny))
 
-    for load in loads:
+    for load in small + loads:
         load.start()
 
     def one(flag):
@@ -215,6 +233,8 @@
             for y in (0, ly + PAD):
                 ref[x, pl.ds(y, PAD)] = jnp.zeros((PAD, nz), f32)
 
+    for load in small:
+        load.wait()
     grid_y = ly * ny
     wcell = wcell_ref[...].reshape(1, -1)
     scell = scell_ref[...].reshape(1, -1)
@@ -440,20 +460,21 @@
     wide = pltpu.VMEM((lx + 2 * RIM, rows, nz), jnp.float32)
     block = pltpu.VMEM((lx, ly, nz), jnp.float32)
     field = jax.ShapeDtypeStruct((lx, ly, nz), jnp.float32)
-    anywhere = pl.BlockSpec(memory_space=pl.ANY)
+    hbm = pl.BlockSpec(memory_space=pltpu.HBM)
     vmem = pl.BlockSpec(memory_space=pltpu.VMEM)
     smem = pl.BlockSpec(memory_space=pltpu.SMEM)
     dma = pltpu.SemaphoreType.DMA
     return pl.pallas_call(
         functools.partial(kernel, nx, ny),
         out_shape=(field, field, field, jax.ShapeDtypeStruct((1,), jnp.float32)),
-        in_specs=[anywhere] * 4 + [vmem] * 5 + [smem],
+        in_specs=[hbm] * 9 + [smem],
         out_specs=(vmem, vmem, vmem, smem),
         scratch_shapes=[wide] * 9
         + [pltpu.VMEM((lx + 2, rows, nz), jnp.float32)]
         + [block] * 4
+        + [pltpu.VMEM(a.shape, a.dtype) for a in args[4:9]]
         + [pltpu.VMEM((ny, 8, nz), jnp.float32), pltpu.VMEM((nx, 8, nz), jnp.float32)]
-        + [dma((4,)), dma((16,)), dma((16,)), dma((8,)), dma((8,))]
+        + [dma((9,)), dma((16,)), dma((16,)), dma((8,)), dma((8,))]
         + [dma((ny,)), dma((ny,)), dma((nx,)), dma((nx,))],
         compiler_params=pltpu.CompilerParams(
             collective_id=0, has_side_effects=True, vmem_limit_bytes=40 * 1024 * 1024

time: 33.1 us -> 33.2 us (level)
  no operation moved by 1% of the time
where the time goes in v2:
time: 33.2 us; the launch traced here: 32.8 us
  Pallas kernels  21.1 us (64%)
  local copies, waits for them, and re-layouts  8.56 us (26%)
  between operations  3.11 us (9%)
    pallas_call x1, Pallas kernels, on_device(): pl.pallas_call(functools.partial(kernel, nx, ny), out_shape=(field, field...  21.1 us
    unnamed x21, local copies, waits for them, and re-layouts  8.56 us

profile of v2, /device:TPU:0, one launch (start us, length us, event | category | flops | bytes accessed | tf_op | source)
XLA Modules:
  0.0 32.8 jit_solution(17275400648347966140)
XLA Ops:
  0.6 0.0 copy-start.7
  0.6 0.0 copy-start.4
  1.3 0.0 copy-done.7
  1.3 0.0 copy-done.4
  1.3 0.0 copy-start
  1.3 1.0 %copy-done = f32[8,128,128]{2,1,0:T(8,128)S(1)} copy-done((f32[8,128,128]{2,1,0:T(8,128)S(1)}, f32[8,128,128]{2,1,0:T(8,128)}, u32[]{:S(2)}) %copy-start) | copy-done | bytes 524312
  2.4 0.0 copy-start.1
  2.4 1.0 %copy-done.1 = f32[8,128,128]{2,1,0:T(8,128)S(1)} copy-done((f32[8,128,128]{2,1,0:T(8,128)S(1)}, f32[8,128,128]{2,1,0:T(8,128)}, u32[]{:S(2)}) %copy-start.1) | copy-done | bytes 524312
  3.4 0.0 copy-start.2
  3.4 1.0 %copy-done.2 = f32[8,128,128]{2,1,0:T(8,128)S(1)} copy-done((f32[8,128,128]{2,1,0:T(8,128)S(1)}, f32[8,128,128]{2,1,0:T(8,128)}, u32[]{:S(2)}) %copy-start.2) | copy-done | bytes 524312
  4.5 0.0 copy-start.3
  4.5 1.0 %copy-done.3 = f32[8,128,128]{2,1,0:T(8,128)S(1)} copy-done((f32[8,128,128]{2,1,0:T(8,128)S(1)}, f32[8,128,128]{2,1,0:T(8,128)}, u32[]{:S(2)}) %copy-start.3) | copy-done | bytes 524312
  5.5 0.0 copy-start.5
  5.5 0.7 %copy-done.5 = f32[256]{0:T(256)S(1)} copy-done((f32[256]{0:T(256)S(1)}, f32[256]{0:T(256)}, u32[]{:S(2)}) %copy-start.5) | copy-done | bytes 1048
  6.2 0.0 copy-start.6
  6.2 0.7 %copy-done.6 = f32[256]{0:T(256)S(1)} copy-done((f32[256]{0:T(256)S(1)}, f32[256]{0:T(256)}, u32[]{:S(2)}) %copy-start.6) | copy-done | bytes 1048
  6.9 0.0 copy-start.8
  6.9 0.7 %copy-done.8 = f32[64]{0:T(128)S(1)} copy-done((f32[64]{0:T(128)S(1)}, f32[64]{0:T(128)}, u32[]{:S(2)}) %copy-start.8) | copy-done | bytes 280
  7.5 21.1 %shard_map.129 = (f32[8,128,128]{2,1,0:T(8,128)S(1)}, f32[8,128,128]{2,1,0:T(8,128)S(1)}, f32[8,128,128]{2,1,0:T(8,128)S(1)}, f32[1]{0:T(128)}) custom-call(f32[8,128,128]{2,1,0:T(8,128)S(1)} %copy-done, f32[8,128,128]{2,1,0:T(8,128)S(1)} %copy-done.1, f32[8,128,128]{2,1,0:T(8,128)S(1)} %copy-done.2, f32[8,128,128]{2,1,0:T(8,128)S(1)} %copy-done.3, ...), custom_call_target="tpu_custom_call" | custom-call | tf_op jit(solution)/shard_map/pallas_call | solution.py:467
  28.6 0.8 %copy.19 = f32[8,128,128]{2,1,0:T(8,128)} copy(f32[8,128,128]{2,1,0:T(8,128)S(1)} %get-tuple-element.8) | data formatting | bytes 1048576
  29.4 0.8 %copy.20 = f32[8,128,128]{2,1,0:T(8,128)} copy(f32[8,128,128]{2,1,0:T(8,128)S(1)} %get-tuple-element.9) | data formatting | bytes 1048576
  30.2 0.8 %copy.21 = f32[8,128,128]{2,1,0:T(8,128)} copy(f32[8,128,128]{2,1,0:T(8,128)S(1)} %get-tuple-element.10) | data formatting | bytes 1048576
Async XLA Ops:
  0.6 0.7 %copy-start.7 = (s32[64]{0:T(128)S(1)}, s32[64]{0:T(128)}, u32[]{:S(2)}) copy-start(s32[64]{0:T(128)} %scell_hbm.1) | copy-start | bytes 772
  0.6 0.7 %copy-start.4 = (s32[256]{0:T(256)S(1)}, s32[256]{0:T(256)}, u32[]{:S(2)}) copy-start(s32[256]{0:T(256)} %wcell_hbm.1) | copy-start | bytes 3076
  1.3 1.0 %copy-start = (f32[8,128,128]{2,1,0:T(8,128)S(1)}, f32[8,128,128]{2,1,0:T(8,128)}, u32[]{:S(2)}) copy-start(f32[8,128,128]{2,1,0:T(8,128)} %lc_ref.1) | copy-start | bytes 1572868
  2.4 1.0 %copy-start.1 = (f32[8,128,128]{2,1,0:T(8,128)S(1)}, f32[8,128,128]{2,1,0:T(8,128)}, u32[]{:S(2)}) copy-start(f32[8,128,128]{2,1,0:T(8,128)} %c_ref.1) | copy-start | bytes 1572868
  3.4 1.0 %copy-start.2 = (f32[8,128,128]{2,1,0:T(8,128)S(1)}, f32[8,128,128]{2,1,0:T(8,128)}, u32[]{:S(2)}) copy-start(f32[8,128,128]{2,1,0:T(8,128)} %survey_ref.1) | copy-start | bytes 1572868
  4.5 1.0 %copy-start.3 = (f32[8,128,128]{2,1,0:T(8,128)S(1)}, f32[8,128,128]{2,1,0:T(8,128)}, u32[]{:S(2)}) copy-start(f32[8,128,128]{2,1,0:T(8,128)} %weight_ref.1) | copy-start | bytes 1572868
  5.5 0.7 %copy-start.5 = (f32[256]{0:T(256)S(1)}, f32[256]{0:T(256)}, u32[]{:S(2)}) copy-start(f32[256]{0:T(256)} %wdata_hbm.1) | copy-start | bytes 3076
  6.2 0.7 %copy-start.6 = (f32[256]{0:T(256)S(1)}, f32[256]{0:T(256)}, u32[]{:S(2)}) copy-start(f32[256]{0:T(256)} %wweight_hbm.1) | copy-start | bytes 3076
  6.9 0.7 %copy-start.8 = (f32[64]{0:T(128)S(1)}, f32[64]{0:T(128)}, u32[]{:S(2)}) copy-start(f32[64]{0:T(128)} %srate_hbm.1) | copy-start | bytes 772

commit v3 on v2

--- a/solution.py
+++ b/solution.py
@@ -63,6 +63,54 @@
     return xs, ys, xd, yd
 
 
+def out_plane(x, c0, c1, a1, a2, fu, fl, ky, kz, ly):
+    v1, v2 = a1[x], a2[x]
+    t0, t1 = c0[x], c1[x]
+    lean = head_slope + dispersivity
+
+    def face_x(p):
+        low1 = lean * c1[p] - dispersivity * c1[p + 1]
+        low0 = lean * c0[p] - dispersivity * c0[p + 1]
+        d1 = a1[p + 1] - a1[p]
+        d2 = a2[p + 1] - a2[p]
+        return (fu[p] - fl[p]) * (d2 * low1 + d1 * low0), d1
+
+    gx_up, above = face_x(x)
+    gx_low, below = face_x(x - 1)
+    grad = gx_up + gx_low
+    new = v1 + (above * fu[x] - below * fl[x - 1])
+    for k, up, down in ((ky[x], up_y, down_y), (kz[x], up_z, down_z)):
+        d1 = up(v1) - v1
+        flow = k * d1
+        new = new + (flow - down(flow))
+        sens = (d1 * (up(t0) - t0) + (up(v2) - v2) * (up(t1) - t1)) * (
+            -0.5 * jnp.maximum(k - time_step * molecular, 0.0)
+        )
+        grad = grad + (sens + down(sens))
+    return grad[PAD : PAD + ly], new[PAD : PAD + ly]
+
+
+def finish(c0, c1, a1, a2, fu, fl, ky, kz, grad_in, adj_in, conc_in, grad, adj, conc, edge, sems):
+    lx, ly, nz = conc.shape
+    mid = pl.ds(2, lx - 4)
+    copies = [
+        pltpu.make_async_copy(conc_in, conc, sems.at[0]),
+        pltpu.make_async_copy(grad_in.at[mid], grad.at[mid], sems.at[1]),
+        pltpu.make_async_copy(adj_in.at[mid], adj.at[mid], sems.at[2]),
+    ]
+    for copy in copies:
+        copy.start()
+    for k, b in enumerate((0, 1, lx - 2, lx - 1)):
+        g, a = out_plane(b + RIM, c0, c1, a1, a2, fu, fl, ky, kz, ly)
+        for slot, value, target in ((2 * k, g, grad), (2 * k + 1, a, adj)):
+            edge[slot] = value
+            copy = pltpu.make_async_copy(edge.at[slot], target.at[b], sems.at[3 + slot])
+            copy.start()
+            copies.append(copy)
+    for copy in copies:
+        copy.wait()
+
+
 def kernel(
     nx,
     ny,
@@ -76,19 +124,19 @@
     scell_hbm,
     srate_hbm,
     step_ref,
+    c0,
+    c1,
+    a1,
+    a2,
+    fu,
+    fl,
+    ky,
+    kz,
     grad_ref,
     adj_ref,
     conc_ref,
     misfit_ref,
     h,
-    c0,
-    c1,
-    a2,
-    a1,
-    fu,
-    fl,
-    ky,
-    kz,
     q,
     ww,
     wd,
@@ -335,32 +383,9 @@
         a1[x] = backward(a2, x)
 
     def do_out(x):
-        b = x - RIM
-        v1, v2 = a1[x], a2[x]
-        t0, t1 = c0[x], c1[x]
-        lean = (head_slope + dispersivity)
-
-        def face_x(p):
-            low1 = lean * c1[p] - dispersivity * c1[p + 1]
-            low0 = lean * c0[p] - dispersivity * c0[p + 1]
-            d1 = a1[p + 1] - a1[p]
-            d2 = a2[p + 1] - a2[p]
-            return (fu[p] - fl[p]) * (d2 * low1 + d1 * low0), d1
-
-        gx_up, above = face_x(x)
-        gx_low, below = face_x(x - 1)
-        grad = gx_up + gx_low
-        new = v1 + (above * fu[x] - below * fl[x - 1])
-        for k, up, down in ((ky[x], up_y, down_y), (kz[x], up_z, down_z)):
-            d1 = up(v1) - v1
-            flow = k * d1
-            new = new + (flow - down(flow))
-            sens = (d1 * (up(t0) - t0) + (up(v2) - v2) * (up(t1) - t1)) * (
-                -0.5 * jnp.maximum(k - time_step * molecular, 0.0)
-            )
-            grad = grad + (sens + down(sens))
-        grad_ref[b] = grad[PAD : PAD + ly]
-        adj_ref[b] = new[PAD : PAD + ly]
+        g, a = out_plane(x, c0, c1, a1, a2, fu, fl, ky, kz, ly)
+        grad_ref[x - RIM] = g
+        adj_ref[x - RIM] = a
 
     def loop(low, high, f):
         @pl.loop(low, high)
@@ -440,8 +465,6 @@
         arrive(second, d)
     for x in (lo - 1, lo, hi - 1, hi):
         do_a1(x)
-    for x in (lo, lo + 1, hi - 2, hi - 1):
-        do_out(x)
 
     reduce_wait(red_x, "gx", i, nx, send_x, recv_x)
     wells = jnp.sum(wweight * wdata * wdata)
@@ -457,29 +480,40 @@
     nx = lax.axis_size("gx")
     ny = lax.axis_size("gy")
     rows = ly + 2 * PAD
-    wide = pltpu.VMEM((lx + 2 * RIM, rows, nz), jnp.float32)
-    block = pltpu.VMEM((lx, ly, nz), jnp.float32)
-    field = jax.ShapeDtypeStruct((lx, ly, nz), jnp.float32)
+    wide = (lx + 2 * RIM, rows, nz)
+    block = (lx, ly, nz)
     hbm = pl.BlockSpec(memory_space=pltpu.HBM)
     vmem = pl.BlockSpec(memory_space=pltpu.VMEM)
     smem = pl.BlockSpec(memory_space=pltpu.SMEM)
     dma = pltpu.SemaphoreType.DMA
-    return pl.pallas_call(
+    f32 = jnp.float32
+    pinned = [pltpu.with_memory_space_constraint(a, pltpu.HBM) for a in args[:9]]
+    *fields, misfit = pl.pallas_call(
         functools.partial(kernel, nx, ny),
-        out_shape=(field, field, field, jax.ShapeDtypeStruct((1,), jnp.float32)),
+        out_shape=[pltpu.VMEM(wide, f32)] * 8
+        + [pltpu.VMEM(block, f32)] * 3
+        + [jax.ShapeDtypeStruct((1,), f32)],
         in_specs=[hbm] * 9 + [smem],
-        out_specs=(vmem, vmem, vmem, smem),
-        scratch_shapes=[wide] * 9
-        + [pltpu.VMEM((lx + 2, rows, nz), jnp.float32)]
-        + [block] * 4
+        out_specs=[vmem] * 11 + [smem],
+        scratch_shapes=[pltpu.VMEM(wide, f32), pltpu.VMEM((lx + 2, rows, nz), f32)]
+        + [pltpu.VMEM(block, f32)] * 4
         + [pltpu.VMEM(a.shape, a.dtype) for a in args[4:9]]
-        + [pltpu.VMEM((ny, 8, nz), jnp.float32), pltpu.VMEM((nx, 8, nz), jnp.float32)]
+        + [pltpu.VMEM((ny, 8, nz), f32), pltpu.VMEM((nx, 8, nz), f32)]
         + [dma((9,)), dma((16,)), dma((16,)), dma((8,)), dma((8,))]
         + [dma((ny,)), dma((ny,)), dma((nx,)), dma((nx,))],
         compiler_params=pltpu.CompilerParams(
-            collective_id=0, has_side_effects=True, vmem_limit_bytes=40 * 1024 * 1024
+            collective_id=0, has_side_effects=True, vmem_limit_bytes=24 * 1024 * 1024
         ),
-    )(*args)
+    )(*pinned, args[9])
+    grad, adj, conc = pl.pallas_call(
+        finish,
+        out_shape=[pltpu.HBM(block, f32)] * 3,
+        in_specs=[vmem] * 11,
+        out_specs=[hbm] * 3,
+        scratch_shapes=[pltpu.VMEM((8, ly, nz), f32), dma((11,))],
+        compiler_params=pltpu.CompilerParams(vmem_limit_bytes=24 * 1024 * 1024),
+    )(*fields)
+    return grad, adj, conc, misfit
 
 
 def solution(mesh):

time: 33.2 us -> 26.4 us (0.80)
  local copies, waits for them, and re-layouts: 8.56 us -> 0 us
  Pallas kernels: 21.1 us -> 23.1 us
    unnamed x21 -> x0, local copies, waits for them, and re-layouts: 8.56 us -> none
    pallas_call x1 -> x2, Pallas kernels: 21.1 us -> 23.1 us  [the longest x1 21.4 us: on_device(): pl.pallas_call(functools.partial(kernel, nx, ny), out_shape=[pltpu.VMEM(w...]
where the time goes in v3:
time: 26.4 us; the launch traced here: 26.2 us
  Pallas kernels  23.1 us (88%)
  between operations  3.05 us (12%)
    pallas_call x1, Pallas kernels, on_device(): pl.pallas_call(functools.partial(kernel, nx, ny), out_shape=[pltpu.VMEM(w...  21.4 us
    pallas_call x1, Pallas kernels, on_device(): pl.pallas_call(finish, out_shape=[pltpu.HBM(block, f32)] * 3, in_specs=[v...  1.74 us

profile of v3, /device:TPU:0, one launch (start us, length us, event | category | flops | bytes accessed | tf_op | source)
XLA Modules:
  0.0 26.2 jit_solution(8910172403381159328)
XLA Ops:
  1.3 21.4 %shard_map.129 = (f32[12,144,128]{2,1,0:T(8,128)S(1)}, f32[12,144,128]{2,1,0:T(8,128)S(1)}, f32[12,144,128]{2,1,0:T(8,128)S(1)}, f32[12,144,128]{2,1,0:T(8,128)S...) custom-call(f32[8,128,128]{2,1,0:T(8,128)} %lc_ref.1, ...), custom_call_target="tpu_custom_call" | custom-call | tf_op jit(solution)/shard_map/pallas_call | solution.py:491
  22.7 1.7 %shard_map.130 = (f32[8,128,128]{2,1,0:T(8,128)}, f32[8,128,128]{2,1,0:T(8,128)}, f32[8,128,128]{2,1,0:T(8,128)}) custom-call(f32[12,144,128]{2,1,0:T(8,128)S(1)} %get-tuple-element.19.c0, f32[12,144,128]{2,1,0:T(8,128)S(1)} %get-tuple-element.20.c1, f32[12,144,128]{2,1,0:T(8,128)S(1)} %get-tuple-element.21.a1, f32[12,144,128]{2,1,0:T(8,128)S(1)} %get-tuple-element.22.a2, ...), custom_call_target="tpu_custom_call" | custom-call | tf_op jit(solution)/shard_map/pallas_call | solution.py:508

commit v4 on v3

--- a/solution.py
+++ b/solution.py
@@ -12,7 +12,7 @@
 molecular = 0.05
 dispersivity = 0.1
 
-RIM = 2
+RIM = 1
 PAD = 8
 DIRS = ((1, 0), (-1, 0), (0, 1), (0, -1), (1, 1), (1, -1), (-1, 1), (-1, -1))
 MESH = pl.DeviceIdType.MESH
@@ -47,7 +47,7 @@
 
 
 def source_slices(dx, dy, lx, ly):
-    width = RIM if dy == 0 else 1
+    width = RIM
     if dx == 0:
         xs, xd = (0, lx), RIM
     elif dx > 0:
@@ -92,7 +92,7 @@
 
 def finish(c0, c1, a1, a2, fu, fl, ky, kz, grad_in, adj_in, conc_in, grad, adj, conc, edge, sems):
     lx, ly, nz = conc.shape
-    mid = pl.ds(2, lx - 4)
+    mid = pl.ds(1, lx - 2)
     copies = [
         pltpu.make_async_copy(conc_in, conc, sems.at[0]),
         pltpu.make_async_copy(grad_in.at[mid], grad.at[mid], sems.at[1]),
@@ -100,7 +100,7 @@
     ]
     for copy in copies:
         copy.start()
-    for k, b in enumerate((0, 1, lx - 2, lx - 1)):
+    for k, b in enumerate((0, lx - 1)):
         g, a = out_plane(b + RIM, c0, c1, a1, a2, fu, fl, ky, kz, ly)
         for slot, value, target in ((2 * k, g, grad), (2 * k + 1, a, adj)):
             edge[slot] = value
@@ -142,6 +142,8 @@
     wd,
     sv,
     sw,
+    part,
+    part_a,
     wcell_ref,
     wdata_ref,
     wweight_ref,
@@ -154,6 +156,8 @@
     recv1,
     send2,
     recv2,
+    send_p,
+    recv_p,
     send_y,
     recv_y,
     send_x,
@@ -238,6 +242,20 @@
     ]
     second = [[remote(d, a2, a2, RIM, PAD, send2.at[d], recv2.at[d])] for d in range(8)]
 
+    def partial_copy(k, src, dst):
+        up = k % 2 == 0
+        return pltpu.make_async_remote_copy(
+            src_ref=src.at[k % 2],
+            dst_ref=dst.at[0 if up else lx + RIM, pl.ds(PAD, ly)],
+            send_sem=send_p.at[k],
+            recv_sem=recv_p.at[k],
+            device_id={"gx": i + 1 if up else i - 1, "gy": j},
+            device_id_type=MESH,
+        )
+
+    third = [[partial_copy(k, part, c1)] for k in range(2)]
+    fourth = [[partial_copy(2 + k, part_a, a1)] for k in range(2)]
+
     def start(copies, d):
         dx, dy = DIRS[d]
 
@@ -275,8 +293,8 @@
                 ref[pl.ds(xd, xs[1]), pl.ds(yd, ys[1])] = jnp.zeros((xs[1], ys[1], nz), f32)
 
     for d in range(8):
-        fill(d, (c0, h, a2))
-    for ref in (c0, h, a2):
+        fill(d, (c0, h, a2) if d > 1 else (c0, h, a2, c1, a1))
+    for ref in (c1, a1):
         for x in (0, lx + 2 * RIM - 1):
             for y in (0, ly + PAD):
                 ref[x, pl.ds(y, PAD)] = jnp.zeros((PAD, nz), f32)
@@ -304,16 +322,14 @@
     well_iota = lax.broadcasted_iota(jnp.int32, (ly, nobs), 0)
     src_iota = lax.broadcasted_iota(jnp.int32, (rows, nsrc), 0) - PAD
 
-    @pl.loop(0, lx)
-    def _(x):
+    def place_wells(x):
         hot = jnp.where(well_iota == well_row - x * grid_y, 1.0, 0.0).astype(jnp.bfloat16)
         both = dot_t(hot, well_parts[0]) + dot_t(hot, well_parts[1]) + dot_t(hot, well_parts[2])
         ww[x] = both[:, :nz]
         wd[x] = both[:, nz:]
 
-    @pl.loop(0, lx + 2)
-    def _(x):
-        hot = jnp.where(src_iota == src_row - (x - 1) * grid_y, 1.0, 0.0).astype(jnp.bfloat16)
+    def place_sources(x):
+        hot = jnp.where(src_iota == src_row - x * grid_y, 1.0, 0.0).astype(jnp.bfloat16)
         parts = dot_t(hot, src_parts)
         q[x] = parts[:, :nz] + parts[:, nz : 2 * nz] + parts[:, 2 * nz :]
 
@@ -365,10 +381,10 @@
         return v + ((above * fu[x] - below * fl[x - 1]) + spread_yz(v, x))
 
     def do_c1(x):
-        c1[x] = forward(c0, x) + gain_first * q[x - 1]
+        c1[x] = forward(c0, x) + gain_first * q[x - RIM]
 
     def do_c2(x, total):
-        final = (forward(c1, x) + gain_second * q[x - 1])[PAD : PAD + ly]
+        final = (forward(c1, x) + gain_second * q[x - RIM])[PAD : PAD + ly]
         b = x - RIM
         conc_ref[b] = final
         missed = final - sv[b]
@@ -395,29 +411,53 @@
     lo, hi = RIM, RIM + lx
     for load in loads:
         load.wait()
-    arrive(first, 2)
-    arrive(first, 3)
-    loop(lo, hi, root)
-    loop(lo, hi, faces_in)
-    loop(lo, hi - 1, faces_x)
+    place_sources(0)
+    place_sources(lx - 1)
+    for d in (2, 3):
+        arrive(first, d)
+    for x in (lo, lo + 1, hi - 2, hi - 1):
+        root(x)
+    for x in (lo, hi - 1):
+        faces_in(x)
+    faces_x(lo)
+    faces_x(hi - 2)
+    v = c0[hi - 1]
+    top = v + (fu[hi - 2] * c0[hi - 2] - fl[hi - 2] * v) + spread_yz(v, hi - 1)
+    c1[hi - 1] = top + gain_first * q[lx - 1]
+    part[0] = c1[hi - 1, pl.ds(PAD, ly)]
+    v = c0[lo]
+    bottom = v - (fu[lo] * v - fl[lo] * c0[lo + 1]) + spread_yz(v, lo)
+    c1[lo] = bottom + gain_first * q[0]
+    part[1] = c1[lo, pl.ds(PAD, ly)]
+    start(third, 0)
+    start(third, 1)
+
+    loop(1, lx - 1, place_sources)
+    loop(lo + 2, hi - 2, root)
+    loop(lo + 1, hi - 1, faces_in)
+    loop(lo + 1, hi - 2, faces_x)
     loop(lo + 1, hi - 1, do_c1)
+    loop(0, lx, place_wells)
     total = lax.fori_loop(lo + 2, hi - 2, do_c2, jnp.zeros((8, nz), f32))
 
     for d in (0, 1, 4, 5, 6, 7):
         arrive(first, d)
-    for x in (lo - 2, lo - 1, hi, hi + 1):
-        root(x)
-    for x in (lo - 1, hi):
-        faces_in(x)
-    for x in (lo - 2, lo - 1, hi - 1, hi):
-        faces_x(x)
-    for x in (lo - 1, lo, hi - 1, hi):
-        do_c1(x)
-    for x in (lo, hi - 1, lo + 1, hi - 2):
-        total = do_c2(x, total)
-
-    for d in (0, 1, 2, 3, 4, 5, 6, 7):
-        start(second, d)
+    root(lo - 1)
+    root(hi)
+    faces_x(lo - 1)
+    faces_x(hi - 1)
+    flux_low = fu[lo - 1] * c0[lo - 1] - fl[lo - 1] * c0[lo]
+    flux_high = fu[hi - 1] * c0[hi - 1] - fl[hi - 1] * c0[hi]
+    c1[lo] = c1[lo] + flux_low
+    c1[hi - 1] = c1[hi - 1] - flux_high
+    total = do_c2(lo + 1, total)
+    total = do_c2(hi - 2, total)
+    arrive(third, 0)
+    arrive(third, 1)
+    c1[lo - 1] = c1[lo - 1] - flux_low
+    c1[hi] = c1[hi] + flux_high
+    total = do_c2(lo, total)
+    total = do_c2(hi - 1, total)
 
     def reduce_start(ref, axis, me, count, send, recv):
         @pl.loop(1, count)
@@ -446,33 +486,49 @@
             copy.wait_send()
             copy.wait_recv()
 
-    red_y[j] = total
-    reduce_start(red_y, "gy", j, ny, send_y, recv_y)
+    red_x[i] = total
+    reduce_start(red_x, "gx", i, nx, send_x, recv_x)
+    for d in (2, 3, 4, 5, 6, 7, 0, 1):
+        start(second, d)
 
     for d in (2, 3):
         arrive(second, d)
-    loop(lo + 2, hi - 2, do_a1)
-
-    reduce_wait(red_y, "gy", j, ny, send_y, recv_y)
-    red_x[i] = jnp.sum(red_y[...], axis=0)
-    reduce_start(red_x, "gx", i, nx, send_x, recv_x)
-
-    do_a1(lo + 1)
-    do_a1(hi - 2)
-    loop(lo + 2, hi - 2, do_out)
+    v = a2[hi - 1]
+    a1[hi - 1] = v - (v - a2[hi - 2]) * fl[hi - 2] + spread_yz(v, hi - 1)
+    part_a[0] = a1[hi - 1, pl.ds(PAD, ly)]
+    v = a2[lo]
+    a1[lo] = v + (a2[lo + 1] - v) * fu[lo] + spread_yz(v, lo)
+    part_a[1] = a1[lo, pl.ds(PAD, ly)]
+    start(fourth, 0)
+    start(fourth, 1)
+
+    loop(lo + 1, hi - 1, do_a1)
+    reduce_wait(red_x, "gx", i, nx, send_x, recv_x)
+    red_y[j] = jnp.sum(red_x[...], axis=0)
+    reduce_start(red_y, "gy", j, ny, send_y, recv_y)
 
     for d in (0, 1, 4, 5, 6, 7):
         arrive(second, d)
-    for x in (lo - 1, lo, hi - 1, hi):
-        do_a1(x)
-
-    reduce_wait(red_x, "gx", i, nx, send_x, recv_x)
+    gap_low = a2[lo] - a2[lo - 1]
+    gap_high = a2[hi] - a2[hi - 1]
+    a1[lo] = a1[lo] - gap_low * fl[lo - 1]
+    a1[hi - 1] = a1[hi - 1] + gap_high * fu[hi - 1]
+    loop(lo + 1, hi - 1, do_out)
+    arrive(fourth, 0)
+    arrive(fourth, 1)
+    a1[lo - 1] = a1[lo - 1] + gap_low * fu[lo - 1]
+    a1[hi] = a1[hi] - gap_high * fl[hi - 1]
+
+    reduce_wait(red_y, "gy", j, ny, send_y, recv_y)
     wells = jnp.sum(wweight * wdata * wdata)
-    whole = jnp.sum(jnp.sum(red_x[...], axis=0)) + wells
+    whole = jnp.sum(jnp.sum(red_y[...], axis=0)) + wells
     misfit_ref[0] = whole * (0.5 / (nx * lx * grid_y * nz))
     for d in range(8):
         sent(first, d)
         sent(second, d)
+    for k in range(2):
+        sent(third, k)
+        sent(fourth, k)
 
 
 def on_device(*args):
@@ -495,11 +551,12 @@
         + [jax.ShapeDtypeStruct((1,), f32)],
         in_specs=[hbm] * 9 + [smem],
         out_specs=[vmem] * 11 + [smem],
-        scratch_shapes=[pltpu.VMEM(wide, f32), pltpu.VMEM((lx + 2, rows, nz), f32)]
+        scratch_shapes=[pltpu.VMEM(wide, f32), pltpu.VMEM((lx, rows, nz), f32)]
         + [pltpu.VMEM(block, f32)] * 4
+        + [pltpu.VMEM((2, ly, nz), f32)] * 2
         + [pltpu.VMEM(a.shape, a.dtype) for a in args[4:9]]
         + [pltpu.VMEM((ny, 8, nz), f32), pltpu.VMEM((nx, 8, nz), f32)]
-        + [dma((9,)), dma((16,)), dma((16,)), dma((8,)), dma((8,))]
+        + [dma((9,)), dma((16,)), dma((16,)), dma((8,)), dma((8,)), dma((4,)), dma((4,))]
         + [dma((ny,)), dma((ny,)), dma((nx,)), dma((nx,))],
         compiler_params=pltpu.CompilerParams(
             collective_id=0, has_side_effects=True, vmem_limit_bytes=24 * 1024 * 1024
@@ -510,7 +567,7 @@
         out_shape=[pltpu.HBM(block, f32)] * 3,
         in_specs=[vmem] * 11,
         out_specs=[hbm] * 3,
-        scratch_shapes=[pltpu.VMEM((8, ly, nz), f32), dma((11,))],
+        scratch_shapes=[pltpu.VMEM((4, ly, nz), f32), dma((7,))],
         compiler_params=pltpu.CompilerParams(vmem_limit_bytes=24 * 1024 * 1024),
     )(*fields)
     return grad, adj, conc, misfit

time: 26.4 us -> 28.2 us (1.068)
  Pallas kernels: 23.1 us -> 25 us
    pallas_call x1, Pallas kernels: 21.4 us -> 23.8 us  [on_device(): pl.pallas_call(functools.partial(kernel, nx, ny), out_shape=[pltpu.VMEM(w...]
    pallas_call x1, Pallas kernels: 1.74 us -> 1.22 us  [on_device(): pl.pallas_call(finish, out_shape=[pltpu.HBM(block, f32)] * 3, in_specs=[v...]
where the time goes in v4:
time: 28.2 us; the launch traced here: 28 us
  Pallas kernels  25 us (89%)
  between operations  3.05 us (11%)
    pallas_call x1, Pallas kernels, on_device(): pl.pallas_call(functools.partial(kernel, nx, ny), out_shape=[pltpu.VMEM(w...  23.8 us
    pallas_call x1, Pallas kernels, on_device(): pl.pallas_call(finish, out_shape=[pltpu.HBM(block, f32)] * 3, in_specs=[v...  1.22 us

profile of v4, /device:TPU:0, one launch (start us, length us, event | category | flops | bytes accessed | tf_op | source)
XLA Modules:
  0.0 28.0 jit_solution(17112147421922039936)
XLA Ops:
  1.3 23.8 %shard_map.129 = (f32[10,144,128]{2,1,0:T(8,128)S(1)}, f32[10,144,128]{2,1,0:T(8,128)S(1)}, f32[10,144,128]{2,1,0:T(8,128)S(1)}, f32[10,144,128]{2,1,0:T(8,128)S...) custom-call(f32[8,128,128]{2,1,0:T(8,128)} %lc_ref.1, ...), custom_call_target="tpu_custom_call" | custom-call | tf_op jit(solution)/shard_map/pallas_call | solution.py:547
  25.0 1.2 %shard_map.130 = (f32[8,128,128]{2,1,0:T(8,128)}, f32[8,128,128]{2,1,0:T(8,128)}, f32[8,128,128]{2,1,0:T(8,128)}) custom-call(f32[10,144,128]{2,1,0:T(8,128)S(1)} %get-tuple-element.19.c0, f32[10,144,128]{2,1,0:T(8,128)S(1)} %get-tuple-element.20.c1, f32[10,144,128]{2,1,0:T(8,128)S(1)} %get-tuple-element.21.a1, f32[10,144,128]{2,1,0:T(8,128)S(1)} %get-tuple-element.22.a2, ...), custom_call_target="tpu_custom_call" | custom-call | tf_op jit(solution)/shard_map/pallas_call | solution.py:565

commit v5 on v4

--- a/solution.py
+++ b/solution.py
@@ -57,9 +57,9 @@
     if dy == 0:
         ys, yd = (0, ly), PAD
     elif dy > 0:
-        ys, yd = (ly - PAD, PAD), 0
+        ys, yd = (ly - 2, 2), PAD - 2
     else:
-        ys, yd = (0, PAD), ly + PAD
+        ys, yd = (0, 2), ly + PAD
     return xs, ys, xd, yd
 
 
@@ -215,6 +215,47 @@
     for load in small + loads:
         load.start()
 
+    grid_y = ly * ny
+    origin = i * lx * grid_y + j * ly
+
+    def hot_rows(cells, count, pad):
+        shape = (lx, count, cells.shape[1])
+        line = lax.broadcasted_iota(jnp.int32, shape, 0) * grid_y + (
+            lax.broadcasted_iota(jnp.int32, shape, 1) - pad
+        )
+        target = lax.div(cells, nz) - origin
+        hot = jnp.where(line == target.reshape(1, 1, -1), 1.0, 0.0)
+        return hot.reshape(lx * count, -1).astype(jnp.bfloat16)
+
+    def hot_lanes(cells, values):
+        shape = (nz, cells.shape[1])
+        at_z = lax.broadcasted_iota(jnp.int32, shape, 0) == lax.rem(cells, nz)
+        return [jnp.where(at_z, p.astype(f32), 0.0).astype(jnp.bfloat16) for p in split3(values)]
+
+    def place_sources():
+        scell = scell_ref[...].reshape(1, -1)
+        srate = srate_ref[...].reshape(1, -1)
+        weights = jnp.concatenate(hot_lanes(scell, srate), axis=0)
+        parts = dot_t(hot_rows(scell, rows, PAD), weights)
+        both = parts[:, :nz] + parts[:, nz : 2 * nz] + parts[:, 2 * nz :]
+        q[...] = both.reshape(lx, rows, nz)
+
+    def place_wells():
+        wcell = wcell_ref[...].reshape(1, -1)
+        wweight = wweight_ref[...].reshape(1, -1)
+        wdata = wdata_ref[...].reshape(1, -1)
+        hot = hot_rows(wcell, ly, 0)
+        for target, values in ((ww, wweight), (wd, wweight * wdata)):
+            weights = jnp.concatenate(hot_lanes(wcell, values), axis=0)
+            parts = dot_t(hot, weights)
+            both = parts[:, :nz] + parts[:, nz : 2 * nz] + parts[:, 2 * nz :]
+            target[...] = both.reshape(lx, ly, nz)
+        return jnp.sum(wweight * wdata * wdata)
+
+    for load in small:
+        load.wait()
+    place_sources()
+
     def one(flag):
         return jnp.where(flag, 1, 0)
 
@@ -298,40 +339,6 @@
         for x in (0, lx + 2 * RIM - 1):
             for y in (0, ly + PAD):
                 ref[x, pl.ds(y, PAD)] = jnp.zeros((PAD, nz), f32)
-
-    for load in small:
-        load.wait()
-    grid_y = ly * ny
-    wcell = wcell_ref[...].reshape(1, -1)
-    scell = scell_ref[...].reshape(1, -1)
-    wweight = wweight_ref[...].reshape(1, -1)
-    wdata = wdata_ref[...].reshape(1, -1)
-    srate = srate_ref[...].reshape(1, -1)
-    nobs, nsrc = wcell.shape[1], scell.shape[1]
-    zi = lax.broadcasted_iota(jnp.int32, (nz, nobs), 0)
-    at_z = zi == lax.rem(wcell, nz)
-    well_parts = []
-    for part_w, part_d in zip(split3(wweight), split3(wweight * wdata)):
-        both = [jnp.where(at_z, p.astype(f32), 0.0).astype(jnp.bfloat16) for p in (part_w, part_d)]
-        well_parts.append(jnp.concatenate(both, axis=0))
-    src_z = lax.broadcasted_iota(jnp.int32, (nz, nsrc), 0) == lax.rem(scell, nz)
-    src_parts = [jnp.where(src_z, p.astype(f32), 0.0).astype(jnp.bfloat16) for p in split3(srate)]
-    src_parts = jnp.concatenate(src_parts, axis=0)
-    well_row = lax.div(wcell, nz) - (i * lx * grid_y + j * ly)
-    src_row = lax.div(scell, nz) - (i * lx * grid_y + j * ly)
-    well_iota = lax.broadcasted_iota(jnp.int32, (ly, nobs), 0)
-    src_iota = lax.broadcasted_iota(jnp.int32, (rows, nsrc), 0) - PAD
-
-    def place_wells(x):
-        hot = jnp.where(well_iota == well_row - x * grid_y, 1.0, 0.0).astype(jnp.bfloat16)
-        both = dot_t(hot, well_parts[0]) + dot_t(hot, well_parts[1]) + dot_t(hot, well_parts[2])
-        ww[x] = both[:, :nz]
-        wd[x] = both[:, nz:]
-
-    def place_sources(x):
-        hot = jnp.where(src_iota == src_row - x * grid_y, 1.0, 0.0).astype(jnp.bfloat16)
-        parts = dot_t(hot, src_parts)
-        q[x] = parts[:, :nz] + parts[:, nz : 2 * nz] + parts[:, 2 * nz :]
 
     clock = jnp.full((1, nz), step_ref[0], jnp.int32).astype(f32)
     gain_first = time_step * (1.0 + 0.5 * jnp.sin(0.05 * clock))
@@ -409,14 +416,22 @@
             f(x)
 
     lo, hi = RIM, RIM + lx
+    wells = place_wells()
     for load in loads:
         load.wait()
-    place_sources(0)
-    place_sources(lx - 1)
+
+    @pl.loop(lo, hi)
+    def _(x):
+        h[x, pl.ds(PAD, ly)] = jnp.exp(0.5 * h[x, pl.ds(PAD, ly)])
+
     for d in (2, 3):
         arrive(first, d)
-    for x in (lo, lo + 1, hi - 2, hi - 1):
-        root(x)
+
+    @pl.loop(lo, hi)
+    def _(x):
+        for y in (0, PAD + ly):
+            h[x, pl.ds(y, PAD)] = jnp.exp(0.5 * h[x, pl.ds(y, PAD)])
+
     for x in (lo, hi - 1):
         faces_in(x)
     faces_x(lo)
@@ -432,12 +447,9 @@
     start(third, 0)
     start(third, 1)
 
-    loop(1, lx - 1, place_sources)
-    loop(lo + 2, hi - 2, root)
     loop(lo + 1, hi - 1, faces_in)
     loop(lo + 1, hi - 2, faces_x)
     loop(lo + 1, hi - 1, do_c1)
-    loop(0, lx, place_wells)
     total = lax.fori_loop(lo + 2, hi - 2, do_c2, jnp.zeros((8, nz), f32))
 
     for d in (0, 1, 4, 5, 6, 7):
@@ -520,7 +532,6 @@
     a1[hi] = a1[hi] - gap_high * fl[hi - 1]
 
     reduce_wait(red_y, "gy", j, ny, send_y, recv_y)
-    wells = jnp.sum(wweight * wdata * wdata)
     whole = jnp.sum(jnp.sum(red_y[...], axis=0)) + wells
     misfit_ref[0] = whole * (0.5 / (nx * lx * grid_y * nz))
     for d in range(8):

time: 28.2 us -> 23.7 us (0.84)
  Pallas kernels: 25 us -> 20.5 us
    pallas_call x1, Pallas kernels: 23.8 us -> 19.3 us  [on_device(): pl.pallas_call(functools.partial(kernel, nx, ny), out_shape=[pltpu.VMEM(w...]
where the time goes in v5:
time: 23.7 us; the launch traced here: 23.5 us
  Pallas kernels  20.5 us (86%)
  between operations  3.05 us (13%)
    pallas_call x1, Pallas kernels, on_device(): pl.pallas_call(functools.partial(kernel, nx, ny), out_shape=[pltpu.VMEM(w...  19.3 us
    pallas_call x1, Pallas kernels, on_device(): pl.pallas_call(finish, out_shape=[pltpu.HBM(block, f32)] * 3, in_specs=[v...  1.22 us

profile of v5, /device:TPU:0, one launch (start us, length us, event | category | flops | bytes accessed | tf_op | source)
XLA Modules:
  0.0 23.5 jit_solution(9714206436389015342)
XLA Ops:
  1.3 19.3 %shard_map.129 = (f32[10,144,128]{2,1,0:T(8,128)S(1)}, f32[10,144,128]{2,1,0:T(8,128)S(1)}, f32[10,144,128]{2,1,0:T(8,128)S(1)}, f32[10,144,128]{2,1,0:T(8,128)S...) custom-call(f32[8,128,128]{2,1,0:T(8,128)} %lc_ref.1, ...), custom_call_target="tpu_custom_call" | custom-call | tf_op jit(solution)/shard_map/pallas_call | solution.py:558
  20.6 1.2 %shard_map.130 = (f32[8,128,128]{2,1,0:T(8,128)}, f32[8,128,128]{2,1,0:T(8,128)}, f32[8,128,128]{2,1,0:T(8,128)}) custom-call(f32[10,144,128]{2,1,0:T(8,128)S(1)} %get-tuple-element.19.c0, f32[10,144,128]{2,1,0:T(8,128)S(1)} %get-tuple-element.20.c1, f32[10,144,128]{2,1,0:T(8,128)S(1)} %get-tuple-element.21.a1, f32[10,144,128]{2,1,0:T(8,128)S(1)} %get-tuple-element.22.a2, ...), custom_call_target="tpu_custom_call" | custom-call | tf_op jit(solution)/shard_map/pallas_call | solution.py:576
